TPU v7x, 256 devices: a whole 4x4x8 slice. The times are simulated.
256 devices in a mesh: cells: 64 (over x, z, core), rhs: 4 (over y).
Axes of the slice: x: 4, y: 4, z: 8, core: 2. Of those that a mesh axis runs over, the one named last changes fastest.
Arguments:
- right_side: bfloat16 [512, 512, 384], P('cells', 'rhs'), may hold values from -6 to 6
- leaf_inverse: bfloat16 [512, 384, 384], P('cells'), may hold values from -0.3125 to 0.3125
- leaf_couple: bfloat16 [512, 9, 384, 128], P('cells'), may hold values from -0.3125 to 0.3125
- skel_target: int32 [512, 9], P('cells'), may hold values from 0 to 2047, as said below
- skeleton_in: float32 [512, 2048, 128], P('rhs', 'cells'), may hold values from -6 to 6
- lift_ops: bfloat16 [64, 4096, 512], P('cells', None, 'rhs'), may hold values from -0.09375 to 0.09375
- node_mix: bfloat16 [64, 1024, 512], P('cells', None, 'rhs'), may hold values from -0.1875 to 0.1875
- node_couple: bfloat16 [64, 512, 512], P('cells', None, 'rhs'), may hold values from -0.125 to 0.125
Outputs:
- leaf_solution: bfloat16 [512, 512, 384], P('cells', 'rhs')
- skeleton_rhs: float32 [512, 2048, 128], P('rhs', 'cells')
- node_solution: bfloat16 [64, 512, 512], P('cells', 'rhs')
- node_skeleton: float32 [64, 512, 512], P('cells', 'rhs')
Inputs may be any that keep to these rules, and one draw needn't show every extreme that they name: `skel_target`: entry (c, k) names a skeleton block; its owner device, the entry // 32, lies at most 2 positions along cells from the cell's device c // 8, and on every device some slot reaches that distance.
All inputs are finite; a program needn't handle non-finite values.
Results may differ from a plain program's by a relative error of at most 0.03.
Values may be sent and summed in bfloat16 or wider, within the bound.
No kernel may reach another device: no remote copies, remote signals or barrier semaphores. Data moves between devices by JAX's collectives and lax.ppermute only.
A program may use at most 128 MiB of HBM per device.

v0:
```python
import jax
import jax.numpy as jnp
from jax import lax
from jax.sharding import PartitionSpec as P

HOP = 2


def passed_along(value, axis, steps):
    count = lax.axis_size(axis)
    initial, last = (max(0, -steps), min(count, count - steps))
    return lax.ppermute(value, axis, [(source, source + steps) for source in range(initial, last)])


def passed_along_2(value, axis, by):
    devices = lax.axis_size(axis)
    return lax.ppermute(value, axis, [(i, (i + by) % devices) for i in range(devices)])


def on_device(
    right_side, leaf_inverse, leaf_couple, skel_target, skeleton_in, lift_ops, node_mix, node_couple
):
    position = lax.axis_index("cells")
    total_devices = lax.axis_size("cells")
    levels = total_devices.bit_length() - 1
    columns = right_side.shape[1]
    blocks = skeleton_in.shape[1]
    block_width = skeleton_in.shape[2]
    solved = jnp.einsum(
        "ncr,nrq->ncq", right_side, leaf_inverse, preferred_element_type=jnp.float32
    ).astype(jnp.bfloat16)
    updates = jnp.einsum("ncr,nkrs->nkcs", solved, leaf_couple, preferred_element_type=jnp.float32)
    slot_count = updates.shape[0] * updates.shape[1]
    updates = updates.reshape(slot_count, columns, block_width)
    targets = skel_target.reshape(slot_count)
    owners = targets // blocks
    within = targets % blocks
    offsets = owners - position
    hop_reach = HOP
    span_rows = 2 * hop_reach + 1
    segment_ids = (offsets + hop_reach) * blocks + within
    summed = jax.ops.segment_sum(updates, segment_ids, num_segments=span_rows * blocks)
    portions = jnp.transpose(summed.reshape(span_rows, blocks, columns, block_width), (0, 2, 1, 3))
    arrived = portions[hop_reach]
    for distance in list(range(-hop_reach, 0)) + list(range(1, hop_reach + 1)):
        arrived = arrived + passed_along(
            portions[hop_reach + distance].astype(jnp.bfloat16), "cells", distance
        ).astype(jnp.float32)
    skeleton_rhs = skeleton_in - arrived
    gathered = (
        lax.all_gather(lift_ops[0], "rhs", axis=1, tiled=True),
        lax.all_gather(node_mix[0], "rhs", axis=1, tiled=True),
        lax.all_gather(node_couple[0], "rhs", axis=1, tiled=True),
    )

    def multiply(operand, which_op):
        return jnp.dot(operand, gathered[which_op], preferred_element_type=jnp.float32)

    def merge_node(left_child, right_child):
        joined = jnp.concatenate([left_child, right_child], axis=1)
        solution = multiply(joined, 1).astype(jnp.bfloat16)
        skeleton = 0.5 * (
            left_child.astype(jnp.float32) + right_child.astype(jnp.float32)
        ) - multiply(solution, 2)
        return (solution, skeleton)

    flattened = skeleton_rhs.reshape(columns, blocks * block_width).astype(jnp.bfloat16)
    current = multiply(flattened, 0).astype(jnp.bfloat16)
    level_solution = jnp.zeros_like(current)
    for section_level in range(1, levels + 1):
        distance = max(1, 2 ** (section_level - 2))
        left_child = passed_along_2(current, "cells", distance)
        if section_level == 1:
            right_child = current
        else:
            right_child = passed_along_2(current, "cells", -distance)
        level_solution, skeleton = merge_node(left_child, right_child)
        current = skeleton.astype(jnp.bfloat16)
    root_pair = passed_along_2(jnp.stack([current, level_solution]), "cells", -(total_devices // 2))
    node_solution, node_skeleton = merge_node(root_pair[0], root_pair[1])
    return (solved, skeleton_rhs, node_solution[None], node_skeleton[None])


def solution(mesh):
    return jax.shard_map(
        on_device,
        mesh=mesh,
        in_specs=(
            P("cells", "rhs", None),
            P("cells", None, None),
            P("cells", None, None, None),
            P("cells", None),
            P("rhs", "cells", None),
            P("cells", None, "rhs"),
            P("cells", None, "rhs"),
            P("cells", None, "rhs"),
        ),
        out_specs=(
            P("cells", "rhs", None),
            P("rhs", "cells", None),
            P("cells", "rhs", None),
            P("cells", "rhs", None),
        ),
        check_vma=False,
    )
```

profile of v0, /device:TPU:32, one launch (start us, length us, event | category | flops | bytes accessed | tf_op | source)
XLA Modules:
  0.0 205.4 jit_solution(803400362444438331)
XLA Ops:
  10.7 7.0 %fusion.27 = f32[8,128,9,128]{3,1,2,0:T(8,128)} fusion(bf16[8,9,384,128]{3,2,1,0:T(8,128)(2,1)} %param.10, bf16[8,128,384]{2,1,0:T(8,128)(2,1)S(1)} %convolution_convert_fusion), kind=kOutput, calls=%fused_computation.34 | convolution fusion | flops 905969664 | bytes 12582912 | tf_op jit(solution)/shard_map/ncr,nkrs->nkcs/dot_general | solution.py:32
  17.7 5.2 %broadcast_in_dim.10 = f32[160,128,128]{2,1,0:T(8,128)} broadcast(f32[]{:T(128)} %constant.30.clone.1), dimensions={} | broadcast | bytes 10485764 | tf_op jit(solution)/shard_map/broadcast_in_dim | solution.py:42
  22.9 17.1 %scatter_fusion = f32[160,128,128]{2,1,0:T(8,128)} fusion(f32[160,128,128]{2,1,0:T(8,128)} %broadcast_in_dim.10, s32[72]{0:T(128)S(1)} %fusion.76, f32[72,128,128]{2,1,0:T(8,128)} %bitcast.121), kind=kCustom, calls=%fused_computation | custom fusion | flops 1179648 | bytes 14156064 | tf_op jit(solution)/shard_map/scatter-add | solution.py:42
  40.0 5.4 %convert.6 = bf16[5,128,32,128]{3,1,2,0:T(8,128)(2,1)S(1)} convert(f32[5,128,32,128]{3,1,2,0:T(8,128)} %bitcast.119) | non-fusion elementwise | flops 2621440 | bytes 15728640 | tf_op jit(solution)/shard_map/convert.3
  47.5 3.9 %collective-permute-start = (bf16[128,32,128]{2,0,1:T(8,128)(2,1)}, bf16[128,32,128]{2,0,1:T(8,128)(2,1)S(1)}, u32[]{:S(2)}, u32[]{:S(2)}) collective-permute-start(bf16[128,32,128]{2,0,1:T(8,128)(2,1)} %get-tuple-element.14), channel_id=1, source_target_pairs={{8,0},{12,4},{16,8},{20,12},{24,16},{28,20},{32,24},{36,28},{40,32... | collective-permute-start | bytes 3145736 | tf_op jit(solution)/shard_map/ppermute | solution.py:12
  57.8 16.8 %collective-permute-done = bf16[128,32,128]{2,0,1:T(8,128)(2,1)S(1)} collective-permute-done((bf16[128,32,128]{2,0,1:T(8,128)(2,1)}, bf16[128,32,128]{2,0,1:T(8,128)(2,1)S(1)}, u32[]{:S(2)}, u32[]{:S(2)}) %collective-permute-start) | collective-permute-done | bytes 1048608 | tf_op jit(solution)/shard_map/ppermute | solution.py:12
  74.5 9.0 %collective-permute-done.1 = bf16[128,32,128]{2,0,1:T(8,128)(2,1)} collective-permute-done((bf16[128,32,128]{2,0,1:T(8,128)(2,1)}, bf16[128,32,128]{2,0,1:T(8,128)(2,1)}, u32[]{:S(2)}, u32[]{:S(2)}) %collective-permute-start.1) | collective-permute-done | bytes 1048608 | tf_op jit(solution)/shard_map/ppermute | solution.py:12
  84.1 6.6 %fusion.119 = (bf16[128,32,128]{2,0,1:T(8,128)(2,1)}, f32[128,32,128]{2,0,1:T(8,128)}) fusion(bf16[128,32,128]{2,0,1:T(8,128)(2,1)} %collective-permute-done.3, bf16[128,32,128]{2,0,1:T(8,128)(2,1)} %collective-permute-done.2, bf16[128,32,128]{2,0,1:T(8,128)(2,1)} %collective-permute-done.1, bf16[128,32,128]{2,0,1:T(8,128)(2,1)S(1)} %collective-permute-done, ...), kind=kLoop, calls=%fused_computation.91 | loop fusion | flops 5242880 | bytes 11534336 | tf_op jit(solution)/shard_map/convert_element_type | solution.py:67
  92.3 2.9 %fusion.7 = bf16[128,512]{1,0:T(8,128)(2,1)S(1)} fusion(bf16[128,4096]{0,1:T(8,128)(2,1)S(1)} %bitcast.122, bf16[1,4096,512]{2,1,0:T(8,128)(2,1)} %all-gather.6.cloned.1.call-done), kind=kOutput, calls=%fused_computation.10 | convolution fusion | flops 536936448 | bytes 5373952 | tf_op jit(solution)/shard_map/dot_general | solution.py:57
  95.3 8.5 %collective-permute-start.4 = (bf16[128,512]{1,0:T(8,128)(2,1)S(1)}, bf16[128,512]{1,0:T(8,128)(2,1)}, u32[]{:S(2)}, u32[]{:S(2)}) collective-permute-start(bf16[128,512]{1,0:T(8,128)(2,1)S(1)} %fusion.7), channel_id=1, source_target_pairs={{0,4},{4,8},{8,12},{12,16},{16,20},{20,24},{24,28},{28,32},{32,36}... | collective-permute-start | bytes 393224 | tf_op jit(solution)/shard_map/ppermute | solution.py:17
  103.7 14.0 %all-gather.2 = bf16[1,512,512]{2,1,0:T(8,128)(2,1)} all-gather(bf16[1,512,128]{2,1,0:T(8,128)(2,1)} %param.15), channel_id=4, replica_groups=mesh['cells'=64,'rhs'=4] {'rhs'}, dimensions={2}, use_global_device_ids=true | all-gather | bytes 655360 | tf_op jit(solution)/shard_map/all_gather | solution.py:53
  117.8 2.6 %subtract_convert_fusion.5 = bf16[128,512]{1,0:T(8,128)(2,1)} fusion(bf16[128,512]{1,0:T(8,128)(2,1)S(1)} %fusion.7, bf16[128,512]{1,0:T(8,128)(2,1)} %collective-permute-done.4, bf16[1,512,512]{2,1,0:T(8,128)(2,1)} %all-gather.2, bf16[1,1024,512]{2,1,0:T(8,128)(2,1)} %all-gather.8.cloned.1.call-done), kind=kOutput, calls=%fused_computation.73 | convolution fusion | flops 202309632 | bytes 1966080 | tf_op jit(solution)/shard_map/dot_general | solution.py:57
  122.2 2.9 %collective-permute-done.5 = bf16[128,512]{1,0:T(8,128)(2,1)S(1)} collective-permute-done((bf16[128,512]{1,0:T(8,128)(2,1)}, bf16[128,512]{1,0:T(8,128)(2,1)S(1)}, u32[]{:S(2)}, u32[]{:S(2)}) %collective-permute-start.5) | collective-permute-done | bytes 131104 | tf_op jit(solution)/shard_map/ppermute | solution.py:17
  125.0 2.6 %subtract_convert_fusion.4 = bf16[128,512]{1,0:T(8,128)(2,1)} fusion(bf16[128,512]{1,0:T(8,128)(2,1)} %collective-permute-done.6, bf16[128,512]{1,0:T(8,128)(2,1)S(1)} %collective-permute-done.5, bf16[1,512,512]{2,1,0:T(8,128)(2,1)} %all-gather.2, bf16[1,1024,512]{2,1,0:T(8,128)(2,1)} %all-gather.8.cloned.1.call-done), kind=kOutput, calls=%fused_computation.72 | convolution fusion | flops 202309632 | bytes 1966080 | tf_op jit(solution)/shard_map/dot_general | solution.py:57
  129.5 3.2 %collective-permute-start.8 = (bf16[128,512]{1,0:T(8,128)(2,1)}, bf16[128,512]{1,0:T(8,128)(2,1)}, u32[]{:S(2)}, u32[]{:S(2)}) collective-permute-start(bf16[128,512]{1,0:T(8,128)(2,1)} %subtract_convert_fusion.4), channel_id=1, source_target_pairs={{0,248},{4,252},{8,0},{12,4},{16,8},{20,12},{24,16},{28,20},{32,24... | collective-permute-start | bytes 393224 | tf_op jit(solution)/shard_map/ppermute | solution.py:17
  132.6 3.2 %collective-permute-done.7 = bf16[128,512]{1,0:T(8,128)(2,1)S(1)} collective-permute-done((bf16[128,512]{1,0:T(8,128)(2,1)}, bf16[128,512]{1,0:T(8,128)(2,1)S(1)}, u32[]{:S(2)}, u32[]{:S(2)}) %collective-permute-start.7) | collective-permute-done | bytes 131104 | tf_op jit(solution)/shard_map/ppermute | solution.py:17
  138.0 10.9 %collective-permute-start.10 = (bf16[128,512]{1,0:T(8,128)(2,1)}, bf16[128,512]{1,0:T(8,128)(2,1)S(1)}, u32[]{:S(2)}, u32[]{:S(2)}) collective-permute-start(bf16[128,512]{1,0:T(8,128)(2,1)} %subtract_convert_fusion.3), channel_id=1, source_target_pairs={{0,240},{4,244},{8,248},{12,252},{16,0},{20,4},{24,8},{28,12},{32,... | collective-permute-start | bytes 393224 | tf_op jit(solution)/shard_map/ppermute | solution.py:17
  148.9 3.2 %collective-permute-done.10 = bf16[128,512]{1,0:T(8,128)(2,1)S(1)} collective-permute-done((bf16[128,512]{1,0:T(8,128)(2,1)}, bf16[128,512]{1,0:T(8,128)(2,1)S(1)}, u32[]{:S(2)}, u32[]{:S(2)}) %collective-permute-start.10) | collective-permute-done | bytes 131104 | tf_op jit(solution)/shard_map/ppermute | solution.py:17
  152.1 7.3 %collective-permute-done.9 = bf16[128,512]{1,0:T(8,128)(2,1)} collective-permute-done((bf16[128,512]{1,0:T(8,128)(2,1)}, bf16[128,512]{1,0:T(8,128)(2,1)}, u32[]{:S(2)}, u32[]{:S(2)}) %collective-permute-start.9) | collective-permute-done | bytes 131104 | tf_op jit(solution)/shard_map/ppermute | solution.py:17
  161.6 8.0 %collective-permute-start.12 = (bf16[128,512]{1,0:T(8,128)(2,1)}, bf16[128,512]{1,0:T(8,128)(2,1)}, u32[]{:S(2)}, u32[]{:S(2)}) collective-permute-start(bf16[128,512]{1,0:T(8,128)(2,1)} %subtract_convert_fusion.2), channel_id=1, source_target_pairs={{0,224},{4,228},{8,232},{12,236},{16,240},{20,244},{24,248},{28,25... | collective-permute-start | bytes 393224 | tf_op jit(solution)/shard_map/ppermute | solution.py:17
  169.7 5.5 %collective-permute-done.11 = bf16[128,512]{1,0:T(8,128)(2,1)S(1)} collective-permute-done((bf16[128,512]{1,0:T(8,128)(2,1)}, bf16[128,512]{1,0:T(8,128)(2,1)S(1)}, u32[]{:S(2)}, u32[]{:S(2)}) %collective-permute-start.11) | collective-permute-done | bytes 131104 | tf_op jit(solution)/shard_map/ppermute | solution.py:17
  175.1 3.4 %collective-permute-done.12 = bf16[128,512]{1,0:T(8,128)(2,1)} collective-permute-done((bf16[128,512]{1,0:T(8,128)(2,1)}, bf16[128,512]{1,0:T(8,128)(2,1)}, u32[]{:S(2)}, u32[]{:S(2)}) %collective-permute-start.12) | collective-permute-done | bytes 131104 | tf_op jit(solution)/shard_map/ppermute | solution.py:17
  184.0 3.2 %collective-permute-done.13 = bf16[128,512]{1,0:T(8,128)(2,1)S(1)} collective-permute-done((bf16[128,512]{1,0:T(8,128)(2,1)}, bf16[128,512]{1,0:T(8,128)(2,1)S(1)}, u32[]{:S(2)}, u32[]{:S(2)}) %collective-permute-start.13) | collective-permute-done | bytes 131104 | tf_op jit(solution)/shard_map/ppermute | solution.py:17
  193.5 3.7 %collective-permute-done.15 = bf16[2,128,512]{2,1,0:T(8,128)(2,1)S(1)} collective-permute-done((bf16[2,128,512]{2,1,0:T(8,128)(2,1)S(1)}, bf16[2,128,512]{2,1,0:T(8,128)(2,1)S(1)}, u32[]{:S(2)}, u32[]{:S(2)}) %collective-permute-start.15) | collective-permute-done | bytes 262176 | tf_op jit(solution)/shard_map/ppermute | solution.py:17
  (50 shorter events, 35.3 us)
Async XLA Ops:
  7.2 1.7 copy-start
  7.2 85.2 %all-gather.6.cloned.1.call-start = ((), (), s32[]{:S(2)}) async-start(), calls=%async_computation | async-start | bytes 5242880 | tf_op jit(solution)/shard_map/all_gather | solution.py:51
  7.9 109.8 %all-gather.8.cloned.1.call-start = ((), (), s32[]{:S(2)}) async-start(), calls=%async_computation.1 | async-start | bytes 1310720 | tf_op jit(solution)/shard_map/all_gather | solution.py:52
  10.7 7.0 %copy-start.4 = (bf16[8,128,384]{2,1,0:T(8,128)(2,1)}, bf16[8,128,384]{2,1,0:T(8,128)(2,1)S(1)}, u32[]{:S(2)}) copy-start(bf16[8,128,384]{2,1,0:T(8,128)(2,1)S(1)} %convolution_convert_fusion) | copy-start | bytes 2359300
  47.5 27.0 %collective-permute-start = (bf16[128,32,128]{2,0,1:T(8,128)(2,1)}, bf16[128,32,128]{2,0,1:T(8,128)(2,1)S(1)}, u32[]{:S(2)}, u32[]{:S(2)}) collective-permute-start(bf16[128,32,128]{2,0,1:T(8,128)(2,1)} %get-tuple-element.14), channel_id=1, source_target_pairs={{8,0},{12,4},{16,8},{20,12},{24,16},{28,20},{32,24},{36,28},{40,32... | collective-permute-start | bytes 3145736 | tf_op jit(solution)/shard_map/ppermute | solution.py:12
  51.5 32.1 %collective-permute-start.1 = (bf16[128,32,128]{2,0,1:T(8,128)(2,1)}, bf16[128,32,128]{2,0,1:T(8,128)(2,1)}, u32[]{:S(2)}, u32[]{:S(2)}) collective-permute-start(bf16[128,32,128]{2,0,1:T(8,128)(2,1)} %get-tuple-element.17), channel_id=1, source_target_pairs={{4,0},{8,4},{12,8},{16,12},{20,16},{24,20},{28,24},{32,28},{36,32}... | collective-permute-start | bytes 3145736 | tf_op jit(solution)/shard_map/ppermute | solution.py:12
  53.4 30.2 %collective-permute-start.2 = (bf16[128,32,128]{2,0,1:T(8,128)(2,1)}, bf16[128,32,128]{2,0,1:T(8,128)(2,1)}, u32[]{:S(2)}, u32[]{:S(2)}) collective-permute-start(bf16[128,32,128]{2,0,1:T(8,128)(2,1)} %get-tuple-element.16), channel_id=1, source_target_pairs={{0,4},{4,8},{8,12},{12,16},{16,20},{20,24},{24,28},{28,32},{32,36}... | collective-permute-start | bytes 3145736 | tf_op jit(solution)/shard_map/ppermute | solution.py:12
  55.8 28.3 %collective-permute-start.3 = (bf16[128,32,128]{2,0,1:T(8,128)(2,1)}, bf16[128,32,128]{2,0,1:T(8,128)(2,1)}, u32[]{:S(2)}, u32[]{:S(2)}) collective-permute-start(bf16[128,32,128]{2,0,1:T(8,128)(2,1)} %get-tuple-element.15), channel_id=1, source_target_pairs={{0,8},{4,12},{8,16},{12,20},{16,24},{20,28},{24,32},{28,36},{32,40... | collective-permute-start | bytes 3145736 | tf_op jit(solution)/shard_map/ppermute | solution.py:12
  95.3 22.5 %collective-permute-start.4 = (bf16[128,512]{1,0:T(8,128)(2,1)S(1)}, bf16[128,512]{1,0:T(8,128)(2,1)}, u32[]{:S(2)}, u32[]{:S(2)}) collective-permute-start(bf16[128,512]{1,0:T(8,128)(2,1)S(1)} %fusion.7), channel_id=1, source_target_pairs={{0,4},{4,8},{8,12},{12,16},{16,20},{20,24},{24,28},{28,32},{32,36}... | collective-permute-start | bytes 393224 | tf_op jit(solution)/shard_map/ppermute | solution.py:17
  117.8 18.0 %copy-start.1 = (bf16[1,1024,512]{2,1,0:T(8,128)(2,1)S(1)}, bf16[1,1024,512]{2,1,0:T(8,128)(2,1)}, u32[]{:S(2)}) copy-start(bf16[1,1024,512]{2,1,0:T(8,128)(2,1)} %all-gather.8.cloned.1.call-done) | copy-start | bytes 3145732
  120.4 4.6 %collective-permute-start.5 = (bf16[128,512]{1,0:T(8,128)(2,1)}, bf16[128,512]{1,0:T(8,128)(2,1)S(1)}, u32[]{:S(2)}, u32[]{:S(2)}) collective-permute-start(bf16[128,512]{1,0:T(8,128)(2,1)} %subtract_convert_fusion.5), channel_id=1, source_target_pairs={{0,4},{4,8},{8,12},{12,16},{16,20},{20,24},{24,28},{28,32},{32,36}... | collective-permute-start | bytes 393224 | tf_op jit(solution)/shard_map/ppermute | solution.py:17
  120.4 4.6 %collective-permute-start.6 = (bf16[128,512]{1,0:T(8,128)(2,1)}, bf16[128,512]{1,0:T(8,128)(2,1)}, u32[]{:S(2)}, u32[]{:S(2)}) collective-permute-start(bf16[128,512]{1,0:T(8,128)(2,1)} %subtract_convert_fusion.5), channel_id=1, source_target_pairs={{0,252},{4,0},{8,4},{12,8},{16,12},{20,16},{24,20},{28,24},{32,28}... | collective-permute-start | bytes 393224 | tf_op jit(solution)/shard_map/ppermute | solution.py:17
  127.6 8.2 %collective-permute-start.7 = (bf16[128,512]{1,0:T(8,128)(2,1)}, bf16[128,512]{1,0:T(8,128)(2,1)S(1)}, u32[]{:S(2)}, u32[]{:S(2)}) collective-permute-start(bf16[128,512]{1,0:T(8,128)(2,1)} %subtract_convert_fusion.4), channel_id=1, source_target_pairs={{0,8},{4,12},{8,16},{12,20},{16,24},{20,28},{24,32},{28,36},{32,40... | collective-permute-start | bytes 393224 | tf_op jit(solution)/shard_map/ppermute | solution.py:17
  129.5 6.3 %collective-permute-start.8 = (bf16[128,512]{1,0:T(8,128)(2,1)}, bf16[128,512]{1,0:T(8,128)(2,1)}, u32[]{:S(2)}, u32[]{:S(2)}) collective-permute-start(bf16[128,512]{1,0:T(8,128)(2,1)} %subtract_convert_fusion.4), channel_id=1, source_target_pairs={{0,248},{4,252},{8,0},{12,4},{16,8},{20,12},{24,16},{28,20},{32,24... | collective-permute-start | bytes 393224 | tf_op jit(solution)/shard_map/ppermute | solution.py:17
  138.0 14.1 %collective-permute-start.10 = (bf16[128,512]{1,0:T(8,128)(2,1)}, bf16[128,512]{1,0:T(8,128)(2,1)S(1)}, u32[]{:S(2)}, u32[]{:S(2)}) collective-permute-start(bf16[128,512]{1,0:T(8,128)(2,1)} %subtract_convert_fusion.3), channel_id=1, source_target_pairs={{0,240},{4,244},{8,248},{12,252},{16,0},{20,4},{24,8},{28,12},{32,... | collective-permute-start | bytes 393224 | tf_op jit(solution)/shard_map/ppermute | solution.py:17
  148.9 10.5 %collective-permute-start.9 = (bf16[128,512]{1,0:T(8,128)(2,1)}, bf16[128,512]{1,0:T(8,128)(2,1)}, u32[]{:S(2)}, u32[]{:S(2)}) collective-permute-start(bf16[128,512]{1,0:T(8,128)(2,1)} %subtract_convert_fusion.3), channel_id=1, source_target_pairs={{0,16},{4,20},{8,24},{12,28},{16,32},{20,36},{24,40},{28,44},{32,4... | collective-permute-start | bytes 393224 | tf_op jit(solution)/shard_map/ppermute | solution.py:17
  161.6 13.5 %collective-permute-start.11 = (bf16[128,512]{1,0:T(8,128)(2,1)}, bf16[128,512]{1,0:T(8,128)(2,1)S(1)}, u32[]{:S(2)}, u32[]{:S(2)}) collective-permute-start(bf16[128,512]{1,0:T(8,128)(2,1)} %subtract_convert_fusion.2), channel_id=1, source_target_pairs={{0,32},{4,36},{8,40},{12,44},{16,48},{20,52},{24,56},{28,60},{32,6... | collective-permute-start | bytes 393224 | tf_op jit(solution)/shard_map/ppermute | solution.py:17
  161.6 16.9 %collective-permute-start.12 = (bf16[128,512]{1,0:T(8,128)(2,1)}, bf16[128,512]{1,0:T(8,128)(2,1)}, u32[]{:S(2)}, u32[]{:S(2)}) collective-permute-start(bf16[128,512]{1,0:T(8,128)(2,1)} %subtract_convert_fusion.2), channel_id=1, source_target_pairs={{0,224},{4,228},{8,232},{12,236},{16,240},{20,244},{24,248},{28,25... | collective-permute-start | bytes 393224 | tf_op jit(solution)/shard_map/ppermute | solution.py:17
  180.8 10.2 %copy-start.3 = (f32[128,32,128]{2,0,1:T(8,128)S(1)}, f32[128,32,128]{2,0,1:T(8,128)}, u32[]{:S(2)}) copy-start(f32[128,32,128]{2,0,1:T(8,128)} %get-tuple-element.13) | copy-start | bytes 6291460
  180.8 6.4 %collective-permute-start.13 = (bf16[128,512]{1,0:T(8,128)(2,1)}, bf16[128,512]{1,0:T(8,128)(2,1)S(1)}, u32[]{:S(2)}, u32[]{:S(2)}) collective-permute-start(bf16[128,512]{1,0:T(8,128)(2,1)} %subtract_convert_fusion.1), channel_id=1, source_target_pairs={{0,64},{4,68},{8,72},{12,76},{16,80},{20,84},{24,88},{28,92},{32,9... | collective-permute-start | bytes 393224 | tf_op jit(solution)/shard_map/ppermute | solution.py:17
  182.4 5.2 %collective-permute-start.14 = (bf16[128,512]{1,0:T(8,128)(2,1)}, bf16[128,512]{1,0:T(8,128)(2,1)S(1)}, u32[]{:S(2)}, u32[]{:S(2)}) collective-permute-start(bf16[128,512]{1,0:T(8,128)(2,1)} %subtract_convert_fusion.1), channel_id=1, source_target_pairs={{0,192},{4,196},{8,200},{12,204},{16,208},{20,212},{24,216},{28,22... | collective-permute-start | bytes 393224 | tf_op jit(solution)/shard_map/ppermute | solution.py:17
  187.9 9.7 %copy-start.2 = (bf16[1,512,512]{2,1,0:T(8,128)(2,1)S(1)}, bf16[1,512,512]{2,1,0:T(8,128)(2,1)}, u32[]{:S(2)}) copy-start(bf16[1,512,512]{2,1,0:T(8,128)(2,1)} %all-gather.2) | copy-start | bytes 1572868
  189.3 8.0 %collective-permute-start.15 = (bf16[2,128,512]{2,1,0:T(8,128)(2,1)S(1)}, bf16[2,128,512]{2,1,0:T(8,128)(2,1)S(1)}, u32[]{:S(2)}, u32[]{:S(2)}) collective-permute-start(bf16[2,128,512]{2,1,0:T(8,128)(2,1)S(1)} %pad_maximum_fusion), channel_id=1, source_target_pairs={{0,128},{4,132},{8,136},{12,140},{16,144},{20,148},{24,152},{28,15... | collective-permute-start | bytes 786440 | tf_op jit(solution)/shard_map/ppermute | solution.py:17
  197.6 1.0 copy-start.5
Sparse Core Ops, SparseCore 0:
  9.8 57.1 all-gather.5
  68.8 29.3 all-gather.7
where the time goes:
time: 208 us; the launch traced here: 205 us
  waiting for transfers between devices  59.7 us (29%)
  starting transfers between devices  49.4 us (24%)
  other arithmetic  29.1 us (14%)
  matrix products  26.6 us (13%)
  between operations  14.2 us (7%)
  blocking collectives  14 us (7%)
  local copies, waits for them, and re-layouts  12.4 us (6%)
    ppermute x12, starting transfers between devices, passed_along_2(): lax.ppermute(value, axis, [(i, (i + by) % devices) for i in range(devices)])  39.2 us
    ppermute x12, waiting for transfers between devices, passed_along_2(): lax.ppermute(value, axis, [(i, (i + by) % devices) for i in range(devices)])  32.6 us
    ppermute x4, waiting for transfers between devices, passed_along(): lax.ppermute(value, axis, [(source, source + steps) for source in range(i...  26.4 us
    dot_general x10, matrix products, multiply(): jnp.dot(operand, gathered[which_op], preferred_element_type=jnp.float32)  17.8 us
    scatter-add x1, other arithmetic, on_device(): jax.ops.segment_sum(updates, segment_ids, num_segments=span_rows * blocks)  17.1 us
    all_gather x1, blocking collectives, on_device(): lax.all_gather(node_couple[0], 'rhs', axis=1, tiled=True)  14 us
    ppermute x4, starting transfers between devices, passed_along(): lax.ppermute(value, axis, [(source, source + steps) for source in range(i...  10.2 us
    dot_general x1, matrix products, on_device(): jnp.einsum('ncr,nkrs->nkcs', solved, leaf_couple, preferred_element_type=...  6.99 us
  transfers between devices with their start and end apart: 18, of which 12 were waited for; matrix products, arithmetic and copies ran while one was open for 26% of the time, Pallas kernels for 0%

commit v1 on v0

v1 whole, which is shorter than its diff:
```python
import functools

import jax
import jax.numpy as jnp
from jax import lax
from jax.experimental import pallas as pl
from jax.experimental.pallas import tpu as pltpu
from jax.sharding import PartitionSpec as P

HOP = 2
BF16 = jnp.bfloat16
F32 = jnp.float32


def dot32(a, b):
    return jnp.dot(a, b, preferred_element_type=F32)


def shifted(value, axis, by):
    count = lax.axis_size(axis)
    return lax.ppermute(value, axis, [(i, (i + by) % count) for i in range(count)])


def along_pairs(value, pairs):
    count = lax.axis_size("cells")
    return lax.ppermute(value, "cells", [(a, b) for a, b in pairs if 0 <= b < count])


def leaf_kernel(slots, blocks, index_ref, roles_ref, rs_ref, inv_ref, couple_ref,
                sol_ref, own_ref, far_ref, near_ref, swap_ref, acc):
    cell = pl.program_id(0)

    @pl.when(cell == 0)
    def _():
        @pl.loop(0, acc.shape[0])
        def _(b):
            acc[b] = jnp.zeros(acc.shape[1:], F32)

    solved = dot32(rs_ref[0], inv_ref[0]).astype(BF16)
    sol_ref[0] = solved
    width = couple_ref.shape[3]
    for first in range(0, slots, 2):
        group = range(first, min(first + 2, slots))
        operators = [couple_ref[0, k] for k in group]
        joined = operators[0] if len(operators) == 1 else jnp.concatenate(operators, axis=1)
        update = dot32(solved, joined)
        for n, k in enumerate(group):
            target = index_ref[cell * slots + k]
            acc[target] += update[:, n * width : (n + 1) * width]

    @pl.when(cell == pl.num_programs(0) - 1)
    def _():
        @pl.loop(0, blocks)
        def _(b):
            own_ref[b] = acc[HOP * blocks + b]
            far_ref[b] = acc[roles_ref[0] * blocks + b].astype(BF16)
            near_ref[b] = acc[roles_ref[1] * blocks + b].astype(BF16)
            swap_ref[0, b] = acc[roles_ref[2] * blocks + b].astype(BF16)
            swap_ref[1, b] = acc[roles_ref[3] * blocks + b].astype(BF16)


def leaf_phase(index, roles, right_side, leaf_inverse, leaf_couple, blocks):
    cells, rows, width = right_side.shape
    slots, sw = leaf_couple.shape[1], leaf_couple.shape[3]
    spans = 2 * HOP + 1
    whole3 = lambda i, *_: (0, 0, 0)
    whole4 = lambda i, *_: (0, 0, 0, 0)
    return pl.pallas_call(
        functools.partial(leaf_kernel, slots, blocks),
        out_shape=(
            jax.ShapeDtypeStruct((cells, rows, width), BF16),
            jax.ShapeDtypeStruct((blocks, rows, sw), F32),
            jax.ShapeDtypeStruct((blocks, rows, sw), BF16),
            jax.ShapeDtypeStruct((blocks, rows, sw), BF16),
            jax.ShapeDtypeStruct((2, blocks, rows, sw), BF16),
        ),
        grid_spec=pltpu.PrefetchScalarGridSpec(
            num_scalar_prefetch=2,
            grid=(cells,),
            in_specs=[
                pl.BlockSpec((1, rows, width), lambda i, *_: (i, 0, 0)),
                pl.BlockSpec((1, width, width), lambda i, *_: (i, 0, 0)),
                pl.BlockSpec((1, slots, width, sw), lambda i, *_: (i, 0, 0, 0)),
            ],
            out_specs=[
                pl.BlockSpec((1, rows, width), lambda i, *_: (i, 0, 0)),
                pl.BlockSpec((blocks, rows, sw), whole3, pipeline_mode=pl.Buffered(1)),
                pl.BlockSpec((blocks, rows, sw), whole3, pipeline_mode=pl.Buffered(1)),
                pl.BlockSpec((blocks, rows, sw), whole3, pipeline_mode=pl.Buffered(1)),
                pl.BlockSpec((2, blocks, rows, sw), whole4, pipeline_mode=pl.Buffered(1)),
            ],
            scratch_shapes=[pltpu.VMEM((spans * blocks, rows, sw), F32)],
        ),
        compiler_params=pltpu.CompilerParams(vmem_limit_bytes=40 << 20),
        cost_estimate=pl.CostEstimate(flops=1_300_000_000, bytes_accessed=17_000_000, transcendentals=0),
        name="leaf",
    )(index, roles, right_side, leaf_inverse, leaf_couple)


def lift_kernel(base_ref, far_ref, near_ref, own_ref, prev_ref, next_ref, opp_lo_ref, opp_hi_ref,
                place_ref, out_ref, acc):
    step = pl.program_id(0)

    @pl.when(step == 0)
    def _():
        acc[...] = jnp.zeros_like(acc)

    count, width = base_ref.shape[1], base_ref.shape[3]
    total = acc[...]
    for half, opp_ref in ((0, opp_lo_ref), (1, opp_hi_ref)):
        parts = []
        for b in range(count):
            value = base_ref[half, b] - far_ref[half, b].astype(F32) - near_ref[half, b].astype(F32)
            parts.append(value.astype(BF16))
        left = jnp.concatenate(parts, axis=1)
        right = jnp.concatenate([own_ref[half], prev_ref[half], next_ref[half], opp_ref[...]], axis=1)
        total = total + dot32(left, right)
    acc[...] = total

    @pl.when(step == pl.num_programs(0) - 1)
    def _():
        sw = own_ref.shape[2]
        for j in range(4):
            at = pl.multiple_of(place_ref[j] * sw, sw)
            out_ref[:, pl.ds(at, sw)] = acc[:, j * sw : (j + 1) * sw].astype(BF16)


def lift_phase(base, far, near, pieces, place):
    own, prev, nxt, opp_lo, opp_hi = pieces
    blocks, rows, width = base.shape
    steps = 4
    per = blocks // 2 // steps
    depth = per * width
    cols = own.shape[1]
    split = lambda v: v.reshape(2, blocks // 2, rows, width)
    halves = lambda v: v.reshape(2, v.shape[0] // 2, cols)
    block_spec = pl.BlockSpec((2, per, rows, width), lambda i: (0, i, 0, 0))
    op_spec = pl.BlockSpec((2, depth, cols), lambda i: (0, i, 0))
    opp_spec = pl.BlockSpec((depth, cols), lambda i: (i, 0))
    return pl.pallas_call(
        lift_kernel,
        out_shape=jax.ShapeDtypeStruct((rows, 4 * cols), BF16),
        grid=(steps,),
        in_specs=[block_spec] * 3 + [op_spec] * 3 + [opp_spec] * 2 + [pl.BlockSpec(memory_space=pltpu.SMEM)],
        out_specs=pl.BlockSpec((rows, 4 * cols), lambda i: (0, 0)),
        scratch_shapes=[pltpu.VMEM((rows, 4 * cols), F32)],
        compiler_params=pltpu.CompilerParams(vmem_limit_bytes=24 << 20),
        cost_estimate=pl.CostEstimate(flops=540_000_000, bytes_accessed=8_000_000, transcendentals=0),
        name="lift",
    )(split(base), split(far), split(near), halves(own), halves(prev), halves(nxt), opp_lo, opp_hi, place)


def assemble_kernel(with_product, own_ref, prev_ref, next_ref, opp_lo_ref, opp_hi_ref, place_ref, ops_ref, *rest):
    sw = own_ref.shape[1]
    half = opp_lo_ref.shape[0]
    for j, ref in enumerate((own_ref, prev_ref, next_ref)):
        ops_ref[:, pl.ds(pl.multiple_of(place_ref[j] * sw, sw), sw)] = ref[...]
    at = pl.multiple_of(place_ref[3] * sw, sw)
    ops_ref[pl.ds(0, half), pl.ds(at, sw)] = opp_lo_ref[...]
    ops_ref[pl.ds(half, half), pl.ds(at, sw)] = opp_hi_ref[...]
    if with_product:
        (product_ref,) = rest
        width = ops_ref.shape[1]
        for r in range(0, 2 * width, width // 2):
            rows = pl.ds(r, width // 2)
            product_ref[rows, :] = (-dot32(ops_ref[rows, :], ops_ref[pl.ds(2 * width, width), :])).astype(BF16)


def assemble(pieces, place, with_product):
    depth, cols = pieces[0].shape
    outs = [jax.ShapeDtypeStruct((depth, 4 * cols), BF16)]
    if with_product:
        outs.append(jax.ShapeDtypeStruct((8 * cols, 4 * cols), BF16))
    vmem = pl.BlockSpec(memory_space=pltpu.VMEM)
    return pl.pallas_call(
        functools.partial(assemble_kernel, with_product),
        out_shape=tuple(outs),
        in_specs=[vmem] * 5 + [pl.BlockSpec(memory_space=pltpu.SMEM)],
        out_specs=tuple([vmem] * len(outs)),
        compiler_params=pltpu.CompilerParams(vmem_limit_bytes=16 << 20),
        cost_estimate=pl.CostEstimate(
            flops=540_000_000 if with_product else 0, bytes_accessed=4_000_000, transcendentals=0
        ),
        name="assemble_product" if with_product else "assemble",
    )(*pieces, place)


def top_kernel(first_ref, second_ref, ops_q_ref, ops_p_ref, sol_ref, skel_ref):
    width = first_ref.shape[1]

    def merge(first, second, ops_ref):
        sol = (dot32(first, ops_ref[pl.ds(0, width), :]) + dot32(second, ops_ref[pl.ds(width, width), :])).astype(BF16)
        skel = 0.5 * (first.astype(F32) + second.astype(F32)) - dot32(sol, ops_ref[pl.ds(2 * width, width), :])
        return sol, skel

    level_sol, level_skel = merge(first_ref[...], second_ref[...], ops_q_ref)
    sol, skel = merge(level_skel.astype(BF16), level_sol, ops_p_ref)
    sol_ref[...] = sol
    skel_ref[...] = skel


def top_phase(first, second, ops_q, ops_p):
    rows, width = first.shape
    vmem = pl.BlockSpec(memory_space=pltpu.VMEM)
    return pl.pallas_call(
        top_kernel,
        out_shape=(jax.ShapeDtypeStruct((rows, width), BF16), jax.ShapeDtypeStruct((rows, width), F32)),
        in_specs=[vmem] * 4,
        out_specs=(vmem, vmem),
        compiler_params=pltpu.CompilerParams(vmem_limit_bytes=16 << 20),
        cost_estimate=pl.CostEstimate(flops=400_000_000, bytes_accessed=4_000_000, transcendentals=0),
        name="top",
    )(first, second, ops_q, ops_p)


def around_rhs(value):
    half = value.shape[0] // 2
    prev = shifted(value, "rhs", 1)
    nxt = shifted(value, "rhs", -1)
    opp_lo = shifted(prev[:half], "rhs", 1)
    opp_hi = shifted(nxt[half:], "rhs", -1)
    return value, prev, nxt, opp_lo, opp_hi


def on_device(
    right_side, leaf_inverse, leaf_couple, skel_target, skeleton_in, lift_ops, node_mix, node_couple
):
    count = lax.axis_size("cells")
    position = lax.axis_index("cells")
    column = lax.axis_index("rhs")
    levels = count.bit_length() - 1
    rows, blocks, width = skeleton_in.shape
    core = position % 2

    place = jnp.stack([column, (column + 3) % 4, (column + 1) % 4, (column + 2) % 4]).astype(jnp.int32)
    lift_pieces = around_rhs(lift_ops[0])
    node_ops = jnp.concatenate([node_mix[0], node_couple[0]], axis=0)
    across = shifted(node_ops, "cells", count // 2)

    targets = skel_target.reshape(-1)
    index = (targets - (position - HOP) * blocks).astype(jnp.int32)
    roles = jnp.where(core == 1, jnp.array([4, 3, 1, 0], jnp.int32), jnp.array([0, 1, 3, 4], jnp.int32))
    solved, own, far, near, swap = leaf_phase(index, roles, right_side, leaf_inverse, leaf_couple, blocks)

    half = range(count // 2)
    far_in = along_pairs(far, [(2 * c + 1, 2 * c + 3) for c in half] + [(2 * c, 2 * c - 2) for c in half])
    swapped = along_pairs(swap, [(2 * c, 2 * c + 1) for c in half] + [(2 * c + 1, 2 * c) for c in half])
    near = (near.astype(F32) + swapped[1].astype(F32)).astype(BF16)
    near_in = along_pairs(near, [(2 * c + 1, 2 * c + 2) for c in half] + [(2 * c, 2 * c - 1) for c in half])

    base = jnp.transpose(skeleton_in, (1, 0, 2)) - own - swapped[0].astype(F32)
    current = lift_phase(base, far_in, near_in, lift_pieces, place)
    final = base - far_in.astype(F32) - near_in.astype(F32)
    skeleton_rhs = jnp.transpose(final, (1, 0, 2))

    ops_p, product = assemble(around_rhs(node_ops), place, True)
    (ops_q,) = assemble(around_rhs(across), place, False)
    mw = current.shape[1]
    for level in range(1, levels):
        distance = max(1, 2 ** (level - 2))
        first = shifted(current, "cells", distance)
        second = current if level == 1 else shifted(current, "cells", -distance)
        skel = 0.5 * (first.astype(F32) + second.astype(F32)) + (
            dot32(first, product[:mw]) + dot32(second, product[mw:])
        )
        current = skel.astype(BF16)
    distance = 2 ** (levels - 2)
    second = shifted(current, "cells", distance)
    first = shifted(current, "cells", -distance)
    node_solution, node_skeleton = top_phase(first, second, ops_q, ops_p)
    return (solved, skeleton_rhs, node_solution[None], node_skeleton[None])


def solution(mesh):
    return jax.shard_map(
        on_device,
        mesh=mesh,
        in_specs=(
            P("cells", "rhs", None),
            P("cells", None, None),
            P("cells", None, None, None),
            P("cells", None),
            P("rhs", "cells", None),
            P("cells", None, "rhs"),
            P("cells", None, "rhs"),
            P("cells", None, "rhs"),
        ),
        out_specs=(
            P("cells", "rhs", None),
            P("rhs", "cells", None),
            P("cells", "rhs", None),
            P("cells", "rhs", None),
        ),
        check_vma=False,
    )
```

time: 208 us -> 162 us (0.78)
  the two profiles are of different devices: /device:TPU:32 before, /device:TPU:1 now
where the time goes in v1:
time: 162 us
  waiting for transfers between devices  76.4 us (47%)
  starting transfers between devices  46.5 us (29%)
  Pallas kernels  18.6 us (11%)
  local copies, waits for them, and re-layouts  10.2 us (6%)
  other arithmetic  6.71 us (4%)
  matrix products  2.31 us (1%)
    ppermute x24, waiting for transfers between devices, shifted(): lax.ppermute(value, axis, [(i, (i + by) % count) for i in range(count)])  76.4 us
    ppermute x24, starting transfers between devices, shifted(): lax.ppermute(value, axis, [(i, (i + by) % count) for i in range(count)])  37.1 us
    pallas_call x1, Pallas kernels, leaf_phase(): pl.pallas_call(functools.partial(leaf_kernel, slots, blocks), out_shape=(...  10.7 us
    ppermute x3, starting transfers between devices, along_pairs(): lax.ppermute(value, 'cells', [(a, b) for a, b in pairs if 0 <= b < count])  9.36 us
    unnamed x23, local copies, waits for them, and re-layouts  7.43 us
    transpose x1, other arithmetic, on_device(): skeleton_rhs = jnp.transpose(final, (1, 0, 2))  3.56 us
    pallas_call x1, Pallas kernels, lift_phase(): pl.pallas_call(lift_kernel, out_shape=jax.ShapeDtypeStruct((rows, 4 * col...  3.44 us
  transfers between devices with their start and end apart: 27, of which 13 were waited for; matrix products, arithmetic and copies ran while one was open for 8% of the time, Pallas kernels for 2%

profile of v1, /device:TPU:1, one launch (start us, length us, event | category | flops | bytes accessed | tf_op | source)
XLA Modules:
  0.0 161.8 jit_solution(9896044065296917931)
XLA Ops:
  4.9 10.7 %leaf.1 = (bf16[8,128,384]{2,1,0:T(8,128)(2,1)}, f32[32,128,128]{2,1,0:T(8,128)S(1)}, bf16[32,128,128]{2,1,0:T(8,128)(2,1)}, bf16[32,128,128]{2,1,0:T(8,128)(2,1)S(1)}, bf16[2,32,128,128]{3,2,1,0:T(8,128)(2,1)S(1)}) custom-call(s32[72]{0:T(128)S(1)} %sub.26.index_ref, s32[4]{0:T(128)S(1)} %broadcast_select_fusion.roles_ref, ...), custom_call_target="tpu_custom_call" | custom-call | flops 1300000000 | bytes 17000000 | tf_op jit(solution)/shard_map/leaf/pallas_call | solution.py:68
  15.6 3.3 %collective-permute-start = (bf16[2,32,128,128]{3,2,1,0:T(8,128)(2,1)S(1)}, bf16[2,32,128,128]{3,2,1,0:T(8,128)(2,1)S(1)}, u32[]{:S(2)}, u32[]{:S(2)}) collective-permute-start(bf16[2,32,128,128]{3,2,1,0:T(8,128)(2,1)S(1)} %get-tuple-element.15), channel_id=1, source_target_pairs={{0,4},{8,12},{16,20},{24,28},{32,36},{40,44},{48,52},{56,60},{64,6... | collective-permute-start | bytes 6291464 | tf_op jit(solution)/shard_map/ppermute | solution.py:26
  19.0 2.7 %collective-permute-start.4 = (bf16[4096,128]{1,0:T(8,128)(2,1)}, bf16[4096,128]{1,0:T(8,128)(2,1)}, u32[]{:S(2)}, u32[]{:S(2)}) collective-permute-start(bf16[4096,128]{1,0:T(8,128)(2,1)} %bitcast.8), channel_id=1, source_target_pairs={{0,3},{1,0},{2,1},{3,2},{4,7},{5,4},{6,5},{7,6},{8,11},{9,8},{10,9... | collective-permute-start | bytes 3145736 | tf_op jit(solution)/shard_map/ppermute | solution.py:21
  25.3 4.2 %collective-permute-start.2 = (bf16[32,128,128]{2,1,0:T(8,128)(2,1)}, bf16[32,128,128]{2,1,0:T(8,128)(2,1)S(1)}, u32[]{:S(2)}, u32[]{:S(2)}) collective-permute-start(bf16[32,128,128]{2,1,0:T(8,128)(2,1)} %fusion), channel_id=1, source_target_pairs={{4,8},{12,16},{20,24},{28,32},{36,40},{44,48},{52,56},{60,64},{68,... | collective-permute-start | bytes 3145736 | tf_op jit(solution)/shard_map/ppermute | solution.py:26
  29.6 23.9 %collective-permute-done.8.prev_ref = bf16[1536,128]{1,0:T(8,128)(2,1)S(1)} collective-permute-done((bf16[1536,128]{1,0:T(8,128)(2,1)S(1)}, bf16[1536,128]{1,0:T(8,128)(2,1)S(1)}, u32[]{:S(2)}, u32[]{:S(2)}) %collective-permute-start.8) | collective-permute-done | bytes 393248 | tf_op jit(solution)/shard_map/ppermute | solution.py:21
  54.3 9.0 %collective-permute-done.9.next_ref = bf16[1536,128]{1,0:T(8,128)(2,1)S(1)} collective-permute-done((bf16[1536,128]{1,0:T(8,128)(2,1)S(1)}, bf16[1536,128]{1,0:T(8,128)(2,1)S(1)}, u32[]{:S(2)}, u32[]{:S(2)}) %collective-permute-start.9) | collective-permute-done | bytes 393248 | tf_op jit(solution)/shard_map/ppermute | solution.py:21
  64.1 2.6 %collective-permute-start.11 = (bf16[768,128]{1,0:T(8,128)(2,1)}, bf16[768,128]{1,0:T(8,128)(2,1)}, u32[]{:S(2)}, u32[]{:S(2)}) collective-permute-start(bf16[768,128]{1,0:T(8,128)(2,1)} %slice.53), channel_id=1, source_target_pairs={{0,3},{1,0},{2,1},{3,2},{4,7},{5,4},{6,5},{7,6},{8,11},{9,8},{10,9... | collective-permute-start | bytes 589832 | tf_op jit(solution)/shard_map/ppermute | solution.py:21
  72.8 2.1 %assemble_product.1 = (bf16[1536,512]{1,0:T(8,128)(2,1)S(1)}, bf16[1024,512]{1,0:T(8,128)(2,1)S(1)}) custom-call(bf16[1536,128]{1,0:T(8,128)(2,1)S(1)} %pad_maximum_fusion.own_ref, bf16[1536,128]{1,0:T(8,128)(2,1)S(1)} %copy-done.5, bf16[1536,128]{1,0:T(8,128)(2,1)S(1)} %copy-done.7, bf16[768,128]{1,0:T(8,128)(2,1)} %collective-permute-done.10.opp_lo_ref, ...), custom_call_target="tpu_custom_call" | custom-call | flops 540000000 | bytes 4000000 | tf_op jit(solution)/shard_map/assemble_product/pallas_call | solution.py:175
  75.0 3.6 %subtract_bitcast_fusion = (f32[128,32,128]{2,0,1:T(8,128)S(1)}, f32[32,128,128]{2,1,0:T(8,128)S(1)}) fusion(bf16[32,128,128]{2,1,0:T(8,128)(2,1)S(1)} %collective-permute-done.2, bf16[32,128,128]{2,1,0:T(8,128)(2,1)S(1)} %collective-permute-done.1, bf16[2,32,128,128]{3,2,1,0:T(8,128)(2,1)} %copy-done.8, f32[32,128,128]{2,1,0:T(8,128)S(1)} %copy-done.2, ...), kind=kLoop, calls=%fused_computation.4 | loop fusion | flops 3670016 | bytes 11534336 | tf_op jit(solution)/shard_map/transpose | solution.py:254
  78.5 2.5 %collective-permute-done.5.opp_lo_ref = bf16[2048,128]{1,0:T(8,128)(2,1)S(1)} collective-permute-done((bf16[2048,128]{1,0:T(8,128)(2,1)S(1)}, bf16[2048,128]{1,0:T(8,128)(2,1)S(1)}, u32[]{:S(2)}, u32[]{:S(2)}) %collective-permute-start.5) | collective-permute-done | bytes 524320 | tf_op jit(solution)/shard_map/ppermute | solution.py:21
  81.0 3.4 %lift.1 = bf16[128,512]{1,0:T(8,128)(2,1)S(1)} custom-call(f32[2,16,128,128]{3,2,1,0:T(8,128)S(1)} %bitcast.43, bf16[2,16,128,128]{3,2,1,0:T(8,128)(2,1)S(1)} %bitcast.44, bf16[2,16,128,128]{3,2,1,0:T(8,128)(2,1)S(1)} %bitcast.45, bf16[2,2048,128]{2,1,0:T(8,128)(2,1)} %bitcast.7.own_ref, bf16[2,2048,128]{2,1,0:T(8,128)(2,1)S(1)} %bitcast.46, ...), custom_call_target="tpu_custom_call" | custom-call | flops 540000000 | bytes 8000000 | tf_op jit(solution)/shard_map/lift/pallas_call | solution.py:140
  84.4 2.7 %collective-permute-start.7 = (bf16[128,512]{1,0:T(8,128)(2,1)S(1)}, bf16[128,512]{1,0:T(8,128)(2,1)S(1)}, u32[]{:S(2)}, u32[]{:S(2)}) collective-permute-start(bf16[128,512]{1,0:T(8,128)(2,1)S(1)} %lift.1), channel_id=1, source_target_pairs={{0,4},{4,8},{8,12},{12,16},{16,20},{20,24},{24,28},{28,32},{32,36}... | collective-permute-start | bytes 393224 | tf_op jit(solution)/shard_map/ppermute | solution.py:21
  89.4 6.1 %collective-permute-start.13 = (bf16[128,512]{1,0:T(8,128)(2,1)S(1)}, bf16[128,512]{1,0:T(8,128)(2,1)S(1)}, u32[]{:S(2)}, u32[]{:S(2)}) collective-permute-start(bf16[128,512]{1,0:T(8,128)(2,1)S(1)} %add_convert_fusion.4), channel_id=1, source_target_pairs={{0,252},{4,0},{8,4},{12,8},{16,12},{20,16},{24,20},{28,24},{32,28}... | collective-permute-start | bytes 393224 | tf_op jit(solution)/shard_map/ppermute | solution.py:21
  97.7 5.7 %collective-permute-start.15 = (bf16[128,512]{1,0:T(8,128)(2,1)S(1)}, bf16[128,512]{1,0:T(8,128)(2,1)S(1)}, u32[]{:S(2)}, u32[]{:S(2)}) collective-permute-start(bf16[128,512]{1,0:T(8,128)(2,1)S(1)} %add_convert_fusion.3), channel_id=1, source_target_pairs={{0,248},{4,252},{8,0},{12,4},{16,8},{20,12},{24,16},{28,20},{32,24... | collective-permute-start | bytes 393224 | tf_op jit(solution)/shard_map/ppermute | solution.py:21
  103.4 3.0 %collective-permute-done.15 = bf16[128,512]{1,0:T(8,128)(2,1)S(1)} collective-permute-done((bf16[128,512]{1,0:T(8,128)(2,1)S(1)}, bf16[128,512]{1,0:T(8,128)(2,1)S(1)}, u32[]{:S(2)}, u32[]{:S(2)}) %collective-permute-start.15) | collective-permute-done | bytes 131104 | tf_op jit(solution)/shard_map/ppermute | solution.py:21
  106.6 4.8 %collective-permute-done.14 = bf16[128,512]{1,0:T(8,128)(2,1)S(1)} collective-permute-done((bf16[128,512]{1,0:T(8,128)(2,1)S(1)}, bf16[128,512]{1,0:T(8,128)(2,1)S(1)}, u32[]{:S(2)}, u32[]{:S(2)}) %collective-permute-start.14) | collective-permute-done | bytes 131104 | tf_op jit(solution)/shard_map/ppermute | solution.py:21
  111.7 8.2 %collective-permute-done.22.own_ref = bf16[1536,128]{1,0:T(8,128)(2,1)S(1)} collective-permute-done((bf16[1536,128]{1,0:T(8,128)(2,1)S(1)}, bf16[1536,128]{1,0:T(8,128)(2,1)S(1)}, u32[]{:S(2)}, u32[]{:S(2)}) %collective-permute-start.22) | collective-permute-done | bytes 393248 | tf_op jit(solution)/shard_map/ppermute | solution.py:21
  120.5 2.8 %collective-permute-start.24 = (bf16[1536,128]{1,0:T(8,128)(2,1)S(1)}, bf16[1536,128]{1,0:T(8,128)(2,1)S(1)}, u32[]{:S(2)}, u32[]{:S(2)}) collective-permute-start(bf16[1536,128]{1,0:T(8,128)(2,1)S(1)} %collective-permute-done.22.own_ref), channel_id=1, source_target_pairs={{0,3},{1,0},{2,1},{3,2},{4,7},{5,4},{6,5},{7,6},{8,11},{9,8},{10,9... | collective-permute-start | bytes 1179656 | tf_op jit(solution)/shard_map/ppermute | solution.py:21
  123.6 14.6 %collective-permute-done.16 = bf16[128,512]{1,0:T(8,128)(2,1)S(1)} collective-permute-done((bf16[128,512]{1,0:T(8,128)(2,1)S(1)}, bf16[128,512]{1,0:T(8,128)(2,1)S(1)}, u32[]{:S(2)}, u32[]{:S(2)}) %collective-permute-start.16) | collective-permute-done | bytes 131104 | tf_op jit(solution)/shard_map/ppermute | solution.py:21
  138.7 2.7 %collective-permute-start.26 = (bf16[768,128]{1,0:T(8,128)(2,1)S(1)}, bf16[768,128]{1,0:T(8,128)(2,1)S(1)}, u32[]{:S(2)}, u32[]{:S(2)}) collective-permute-start(bf16[768,128]{1,0:T(8,128)(2,1)S(1)} %slice.55), channel_id=1, source_target_pairs={{0,3},{1,0},{2,1},{3,2},{4,7},{5,4},{6,5},{7,6},{8,11},{9,8},{10,9... | collective-permute-start | bytes 589832 | tf_op jit(solution)/shard_map/ppermute | solution.py:21
  141.4 5.3 %collective-permute-start.18 = (bf16[128,512]{1,0:T(8,128)(2,1)S(1)}, bf16[128,512]{1,0:T(8,128)(2,1)S(1)}, u32[]{:S(2)}, u32[]{:S(2)}) collective-permute-start(bf16[128,512]{1,0:T(8,128)(2,1)S(1)} %add_convert_fusion.1), channel_id=1, source_target_pairs={{0,32},{4,36},{8,40},{12,44},{16,48},{20,52},{24,56},{28,60},{32,6... | collective-permute-start | bytes 393224 | tf_op jit(solution)/shard_map/ppermute | solution.py:21
  147.4 5.4 %collective-permute-done.18 = bf16[128,512]{1,0:T(8,128)(2,1)S(1)} collective-permute-done((bf16[128,512]{1,0:T(8,128)(2,1)S(1)}, bf16[128,512]{1,0:T(8,128)(2,1)S(1)}, u32[]{:S(2)}, u32[]{:S(2)}) %collective-permute-start.18) | collective-permute-done | bytes 131104 | tf_op jit(solution)/shard_map/ppermute | solution.py:21
  153.1 3.8 %collective-permute-start.21 = (bf16[128,512]{1,0:T(8,128)(2,1)S(1)}, bf16[128,512]{1,0:T(8,128)(2,1)S(1)}, u32[]{:S(2)}, u32[]{:S(2)}) collective-permute-start(bf16[128,512]{1,0:T(8,128)(2,1)S(1)} %add_convert_fusion), channel_id=1, source_target_pairs={{0,64},{4,68},{8,72},{12,76},{16,80},{20,84},{24,88},{28,92},{32,9... | collective-permute-start | bytes 393224 | tf_op jit(solution)/shard_map/ppermute | solution.py:21
  157.7 2.5 %copy.15 = f32[128,32,128]{2,1,0:T(8,128)} copy(f32[128,32,128]{2,0,1:T(8,128)S(1)} %get-tuple-element.26) | data formatting | bytes 4194304
  (81 shorter events, 25.1 us)
Async XLA Ops:
  15.6 7.9 %collective-permute-start = (bf16[2,32,128,128]{3,2,1,0:T(8,128)(2,1)S(1)}, bf16[2,32,128,128]{3,2,1,0:T(8,128)(2,1)S(1)}, u32[]{:S(2)}, u32[]{:S(2)}) collective-permute-start(bf16[2,32,128,128]{3,2,1,0:T(8,128)(2,1)S(1)} %get-tuple-element.15), channel_id=1, source_target_pairs={{0,4},{8,12},{16,20},{24,28},{32,36},{40,44},{48,52},{56,60},{64,6... | collective-permute-start | bytes 6291464 | tf_op jit(solution)/shard_map/ppermute | solution.py:26
  19.0 45.1 %collective-permute-start.3 = (bf16[4096,128]{1,0:T(8,128)(2,1)}, bf16[4096,128]{1,0:T(8,128)(2,1)S(1)}, u32[]{:S(2)}, u32[]{:S(2)}) collective-permute-start(bf16[4096,128]{1,0:T(8,128)(2,1)} %bitcast.8), channel_id=1, source_target_pairs={{0,1},{1,2},{2,3},{3,0},{4,5},{5,6},{6,7},{7,4},{8,9},{9,10},{10,1... | collective-permute-start | bytes 3145736 | tf_op jit(solution)/shard_map/ppermute | solution.py:21
  19.0 47.9 %collective-permute-start.4 = (bf16[4096,128]{1,0:T(8,128)(2,1)}, bf16[4096,128]{1,0:T(8,128)(2,1)}, u32[]{:S(2)}, u32[]{:S(2)}) collective-permute-start(bf16[4096,128]{1,0:T(8,128)(2,1)} %bitcast.8), channel_id=1, source_target_pairs={{0,3},{1,0},{2,1},{3,2},{4,7},{5,4},{6,5},{7,6},{8,11},{9,8},{10,9... | collective-permute-start | bytes 3145736 | tf_op jit(solution)/shard_map/ppermute | solution.py:21
  21.6 53.3 %collective-permute-start.1 = (bf16[32,128,128]{2,1,0:T(8,128)(2,1)}, bf16[32,128,128]{2,1,0:T(8,128)(2,1)S(1)}, u32[]{:S(2)}, u32[]{:S(2)}) collective-permute-start(bf16[32,128,128]{2,1,0:T(8,128)(2,1)} %get-tuple-element.16), channel_id=1, source_target_pairs={{4,12},{12,20},{20,28},{28,36},{36,44},{44,52},{52,60},{60,68},{68... | collective-permute-start | bytes 3145736 | tf_op jit(solution)/shard_map/ppermute | solution.py:26
  25.3 49.7 %collective-permute-start.2 = (bf16[32,128,128]{2,1,0:T(8,128)(2,1)}, bf16[32,128,128]{2,1,0:T(8,128)(2,1)S(1)}, u32[]{:S(2)}, u32[]{:S(2)}) collective-permute-start(bf16[32,128,128]{2,1,0:T(8,128)(2,1)} %fusion), channel_id=1, source_target_pairs={{4,8},{12,16},{20,24},{28,32},{36,40},{44,48},{52,56},{60,64},{68,... | collective-permute-start | bytes 3145736 | tf_op jit(solution)/shard_map/ppermute | solution.py:26
  29.5 24.0 %collective-permute-start.8 = (bf16[1536,128]{1,0:T(8,128)(2,1)S(1)}, bf16[1536,128]{1,0:T(8,128)(2,1)S(1)}, u32[]{:S(2)}, u32[]{:S(2)}) collective-permute-start(bf16[1536,128]{1,0:T(8,128)(2,1)S(1)} %pad_maximum_fusion.own_ref), channel_id=1, source_target_pairs={{0,1},{1,2},{2,3},{3,0},{4,5},{5,6},{6,7},{7,4},{8,9},{9,10},{10,1... | collective-permute-start | bytes 1179656 | tf_op jit(solution)/shard_map/ppermute | solution.py:21
  53.5 9.8 %collective-permute-start.9 = (bf16[1536,128]{1,0:T(8,128)(2,1)S(1)}, bf16[1536,128]{1,0:T(8,128)(2,1)S(1)}, u32[]{:S(2)}, u32[]{:S(2)}) collective-permute-start(bf16[1536,128]{1,0:T(8,128)(2,1)S(1)} %pad_maximum_fusion.own_ref), channel_id=1, source_target_pairs={{0,3},{1,0},{2,1},{3,2},{4,7},{5,4},{6,5},{7,6},{8,11},{9,8},{10,9... | collective-permute-start | bytes 1179656 | tf_op jit(solution)/shard_map/ppermute | solution.py:21
  64.1 6.7 %collective-permute-start.11 = (bf16[768,128]{1,0:T(8,128)(2,1)}, bf16[768,128]{1,0:T(8,128)(2,1)}, u32[]{:S(2)}, u32[]{:S(2)}) collective-permute-start(bf16[768,128]{1,0:T(8,128)(2,1)} %slice.53), channel_id=1, source_target_pairs={{0,3},{1,0},{2,1},{3,2},{4,7},{5,4},{6,5},{7,6},{8,11},{9,8},{10,9... | collective-permute-start | bytes 589832 | tf_op jit(solution)/shard_map/ppermute | solution.py:21
  66.9 14.1 %collective-permute-start.5 = (bf16[2048,128]{1,0:T(8,128)(2,1)S(1)}, bf16[2048,128]{1,0:T(8,128)(2,1)S(1)}, u32[]{:S(2)}, u32[]{:S(2)}) collective-permute-start(bf16[2048,128]{1,0:T(8,128)(2,1)S(1)} %slice.50), channel_id=1, source_target_pairs={{0,1},{1,2},{2,3},{3,0},{4,5},{5,6},{6,7},{7,4},{8,9},{9,10},{10,1... | collective-permute-start | bytes 1572872 | tf_op jit(solution)/shard_map/ppermute | solution.py:21
  69.3 11.7 %collective-permute-start.6 = (bf16[2048,128]{1,0:T(8,128)(2,1)S(1)}, bf16[2048,128]{1,0:T(8,128)(2,1)S(1)}, u32[]{:S(2)}, u32[]{:S(2)}) collective-permute-start(bf16[2048,128]{1,0:T(8,128)(2,1)S(1)} %slice.51), channel_id=1, source_target_pairs={{0,3},{1,0},{2,1},{3,2},{4,7},{5,4},{6,5},{7,6},{8,11},{9,8},{10,9... | collective-permute-start | bytes 1572872 | tf_op jit(solution)/shard_map/ppermute | solution.py:21
  89.4 7.1 %collective-permute-start.13 = (bf16[128,512]{1,0:T(8,128)(2,1)S(1)}, bf16[128,512]{1,0:T(8,128)(2,1)S(1)}, u32[]{:S(2)}, u32[]{:S(2)}) collective-permute-start(bf16[128,512]{1,0:T(8,128)(2,1)S(1)} %add_convert_fusion.4), channel_id=1, source_target_pairs={{0,252},{4,0},{8,4},{12,8},{16,12},{20,16},{24,20},{28,24},{32,28}... | collective-permute-start | bytes 393224 | tf_op jit(solution)/shard_map/ppermute | solution.py:21
  97.7 8.7 %collective-permute-start.15 = (bf16[128,512]{1,0:T(8,128)(2,1)S(1)}, bf16[128,512]{1,0:T(8,128)(2,1)S(1)}, u32[]{:S(2)}, u32[]{:S(2)}) collective-permute-start(bf16[128,512]{1,0:T(8,128)(2,1)S(1)} %add_convert_fusion.3), channel_id=1, source_target_pairs={{0,248},{4,252},{8,0},{12,4},{16,8},{20,12},{24,16},{28,20},{32,24... | collective-permute-start | bytes 393224 | tf_op jit(solution)/shard_map/ppermute | solution.py:21
  103.4 16.5 %collective-permute-start.22 = (bf16[1536,128]{1,0:T(8,128)(2,1)S(1)}, bf16[1536,128]{1,0:T(8,128)(2,1)S(1)}, u32[]{:S(2)}, u32[]{:S(2)}) collective-permute-start(bf16[1536,128]{1,0:T(8,128)(2,1)S(1)} %pad_maximum_fusion.own_ref), channel_id=1, source_target_pairs={{0,128},{4,132},{8,136},{12,140},{16,144},{20,148},{24,152},{28,15... | collective-permute-start | bytes 1179656 | tf_op jit(solution)/shard_map/ppermute | solution.py:21
  103.4 8.0 %collective-permute-start.14 = (bf16[128,512]{1,0:T(8,128)(2,1)S(1)}, bf16[128,512]{1,0:T(8,128)(2,1)S(1)}, u32[]{:S(2)}, u32[]{:S(2)}) collective-permute-start(bf16[128,512]{1,0:T(8,128)(2,1)S(1)} %add_convert_fusion.3), channel_id=1, source_target_pairs={{0,8},{4,12},{8,16},{12,20},{16,24},{20,28},{24,32},{28,36},{32,40... | collective-permute-start | bytes 393224 | tf_op jit(solution)/shard_map/ppermute | solution.py:21
  111.6 11.8 %collective-permute-start.17 = (bf16[128,512]{1,0:T(8,128)(2,1)S(1)}, bf16[128,512]{1,0:T(8,128)(2,1)S(1)}, u32[]{:S(2)}, u32[]{:S(2)}) collective-permute-start(bf16[128,512]{1,0:T(8,128)(2,1)S(1)} %add_convert_fusion.2), channel_id=1, source_target_pairs={{0,240},{4,244},{8,248},{12,252},{16,0},{20,4},{24,8},{28,12},{32,... | collective-permute-start | bytes 393224 | tf_op jit(solution)/shard_map/ppermute | solution.py:21
  119.9 18.7 %collective-permute-start.23 = (bf16[1536,128]{1,0:T(8,128)(2,1)S(1)}, bf16[1536,128]{1,0:T(8,128)(2,1)S(1)}, u32[]{:S(2)}, u32[]{:S(2)}) collective-permute-start(bf16[1536,128]{1,0:T(8,128)(2,1)S(1)} %collective-permute-done.22.own_ref), channel_id=1, source_target_pairs={{0,1},{1,2},{2,3},{3,0},{4,5},{5,6},{6,7},{7,4},{8,9},{9,10},{10,1... | collective-permute-start | bytes 1179656 | tf_op jit(solution)/shard_map/ppermute | solution.py:21
  120.5 18.2 %collective-permute-start.24 = (bf16[1536,128]{1,0:T(8,128)(2,1)S(1)}, bf16[1536,128]{1,0:T(8,128)(2,1)S(1)}, u32[]{:S(2)}, u32[]{:S(2)}) collective-permute-start(bf16[1536,128]{1,0:T(8,128)(2,1)S(1)} %collective-permute-done.22.own_ref), channel_id=1, source_target_pairs={{0,3},{1,0},{2,1},{3,2},{4,7},{5,4},{6,5},{7,6},{8,11},{9,8},{10,9... | collective-permute-start | bytes 1179656 | tf_op jit(solution)/shard_map/ppermute | solution.py:21
  123.3 14.9 %collective-permute-start.16 = (bf16[128,512]{1,0:T(8,128)(2,1)S(1)}, bf16[128,512]{1,0:T(8,128)(2,1)S(1)}, u32[]{:S(2)}, u32[]{:S(2)}) collective-permute-start(bf16[128,512]{1,0:T(8,128)(2,1)S(1)} %add_convert_fusion.2), channel_id=1, source_target_pairs={{0,16},{4,20},{8,24},{12,28},{16,32},{20,36},{24,40},{28,44},{32,4... | collective-permute-start | bytes 393224 | tf_op jit(solution)/shard_map/ppermute | solution.py:21
  138.4 8.8 %collective-permute-start.19 = (bf16[128,512]{1,0:T(8,128)(2,1)S(1)}, bf16[128,512]{1,0:T(8,128)(2,1)S(1)}, u32[]{:S(2)}, u32[]{:S(2)}) collective-permute-start(bf16[128,512]{1,0:T(8,128)(2,1)S(1)} %add_convert_fusion.1), channel_id=1, source_target_pairs={{0,224},{4,228},{8,232},{12,236},{16,240},{20,244},{24,248},{28,25... | collective-permute-start | bytes 393224 | tf_op jit(solution)/shard_map/ppermute | solution.py:21
  138.6 18.3 %collective-permute-start.25 = (bf16[768,128]{1,0:T(8,128)(2,1)S(1)}, bf16[768,128]{1,0:T(8,128)(2,1)S(1)}, u32[]{:S(2)}, u32[]{:S(2)}) collective-permute-start(bf16[768,128]{1,0:T(8,128)(2,1)S(1)} %slice.54), channel_id=1, source_target_pairs={{0,1},{1,2},{2,3},{3,0},{4,5},{5,6},{6,7},{7,4},{8,9},{9,10},{10,1... | collective-permute-start | bytes 589832 | tf_op jit(solution)/shard_map/ppermute | solution.py:21
  138.7 18.2 %collective-permute-start.26 = (bf16[768,128]{1,0:T(8,128)(2,1)S(1)}, bf16[768,128]{1,0:T(8,128)(2,1)S(1)}, u32[]{:S(2)}, u32[]{:S(2)}) collective-permute-start(bf16[768,128]{1,0:T(8,128)(2,1)S(1)} %slice.55), channel_id=1, source_target_pairs={{0,3},{1,0},{2,1},{3,2},{4,7},{5,4},{6,5},{7,6},{8,11},{9,8},{10,9... | collective-permute-start | bytes 589832 | tf_op jit(solution)/shard_map/ppermute | solution.py:21
  141.4 11.4 %collective-permute-start.18 = (bf16[128,512]{1,0:T(8,128)(2,1)S(1)}, bf16[128,512]{1,0:T(8,128)(2,1)S(1)}, u32[]{:S(2)}, u32[]{:S(2)}) collective-permute-start(bf16[128,512]{1,0:T(8,128)(2,1)S(1)} %add_convert_fusion.1), channel_id=1, source_target_pairs={{0,32},{4,36},{8,40},{12,44},{16,48},{20,52},{24,56},{28,60},{32,6... | collective-permute-start | bytes 393224 | tf_op jit(solution)/shard_map/ppermute | solution.py:21
  153.0 7.2 %collective-permute-start.20 = (bf16[128,512]{1,0:T(8,128)(2,1)S(1)}, bf16[128,512]{1,0:T(8,128)(2,1)S(1)}, u32[]{:S(2)}, u32[]{:S(2)}) collective-permute-start(bf16[128,512]{1,0:T(8,128)(2,1)S(1)} %add_convert_fusion), channel_id=1, source_target_pairs={{0,192},{4,196},{8,200},{12,204},{16,208},{20,212},{24,216},{28,22... | collective-permute-start | bytes 393224 | tf_op jit(solution)/shard_map/ppermute | solution.py:21
  153.1 7.1 %collective-permute-start.21 = (bf16[128,512]{1,0:T(8,128)(2,1)S(1)}, bf16[128,512]{1,0:T(8,128)(2,1)S(1)}, u32[]{:S(2)}, u32[]{:S(2)}) collective-permute-start(bf16[128,512]{1,0:T(8,128)(2,1)S(1)} %add_convert_fusion), channel_id=1, source_target_pairs={{0,64},{4,68},{8,72},{12,76},{16,80},{20,84},{24,88},{28,92},{32,9... | collective-permute-start | bytes 393224 | tf_op jit(solution)/shard_map/ppermute | solution.py:21
  (14 other events, 143.8 us)

commit v2 on v1

v2 whole, which is shorter than its diff:
```python
import functools

import jax
import jax.numpy as jnp
from jax import lax
from jax.experimental import pallas as pl
from jax.experimental.pallas import tpu as pltpu
from jax.sharding import PartitionSpec as P

HOP = 2
DEST_PARTS = (24, 8)
RED_PARTS = (16, 16)
BF16 = jnp.bfloat16
F32 = jnp.float32


def dot32(a, b):
    return jnp.dot(a, b, preferred_element_type=F32)


def shifted(value, axis, by):
    count = lax.axis_size(axis)
    return lax.ppermute(value, axis, [(i, (i + by) % count) for i in range(count)])


def along_pairs(value, pairs):
    count = lax.axis_size("cells")
    return lax.ppermute(value, "cells", [(a, b) for a, b in pairs if 0 <= b < count])


def copy_parts(acc, start, refs):
    first = 0
    for ref in refs:

        @pl.loop(0, ref.shape[0])
        def _(b, ref=ref, first=first):
            ref[b] = acc[start + first + b].astype(BF16)

        first += ref.shape[0]


def leaf_kernel(cells, slots, blocks, target_ref, rs_ref, inv_ref, couple_ref,
                sol_ref, own_ref, far_ref, near_ref, *refs):
    *part_refs, acc = refs
    step = pl.program_id(0)
    position = lax.axis_index("cells")
    shift = (position - HOP) * blocks

    @pl.when(step == 0)
    def _():
        @pl.loop(0, acc.shape[0])
        def _(b):
            acc[b] = jnp.zeros(acc.shape[1:], F32)

    width = couple_ref.shape[3]
    solved = []
    for c in range(cells):
        value = dot32(rs_ref[c], inv_ref[c]).astype(BF16)
        sol_ref[c] = value
        solved.append(value)
    for c in range(cells):
        for first in range(0, slots, 2):
            group = range(first, min(first + 2, slots))
            operators = [couple_ref[c, k] for k in group]
            joined = operators[0] if len(operators) == 1 else jnp.concatenate(operators, axis=1)
            update = dot32(solved[c], joined)
            for n, k in enumerate(group):
                target = target_ref[step * cells + c, k] - shift
                acc[target] += update[:, n * width : (n + 1) * width]

    @pl.when(step == pl.num_programs(0) - 1)
    def _():
        odd = position % 2
        spans = 2 * HOP
        far, near, dest, red = (
            jnp.where(odd == 1, spans - k, k) * blocks for k in (0, 1, HOP + 1, 2 * HOP)
        )

        @pl.loop(0, blocks)
        def _(b):
            own_ref[b] = acc[HOP * blocks + b]
            far_ref[b] = acc[far + b].astype(BF16)
            near_ref[b] = acc[near + b].astype(BF16)

        copy_parts(acc, dest, part_refs[: len(DEST_PARTS)])
        copy_parts(acc, red, part_refs[len(DEST_PARTS) :])


def leaf_phase(targets, right_side, leaf_inverse, leaf_couple, blocks, per_step=4):
    cells, rows, width = right_side.shape
    slots, sw = leaf_couple.shape[1], leaf_couple.shape[3]
    spans = 2 * HOP + 1
    whole = lambda i, *_: (0, 0, 0)
    by_cell = lambda i, *_: (i, 0, 0)
    summed = pl.BlockSpec((blocks, rows, sw), whole, pipeline_mode=pl.Buffered(1))
    parts = [blocks * n // 32 for n in DEST_PARTS + RED_PARTS]
    return pl.pallas_call(
        functools.partial(leaf_kernel, per_step, slots, blocks),
        out_shape=(
            jax.ShapeDtypeStruct((cells, rows, width), BF16),
            jax.ShapeDtypeStruct((blocks, rows, sw), F32),
        )
        + (jax.ShapeDtypeStruct((blocks, rows, sw), BF16),) * 2
        + tuple(jax.ShapeDtypeStruct((n, rows, sw), BF16) for n in parts),
        grid_spec=pltpu.PrefetchScalarGridSpec(
            num_scalar_prefetch=1,
            grid=(cells // per_step,),
            in_specs=[
                pl.BlockSpec((per_step, rows, width), by_cell),
                pl.BlockSpec((per_step, width, width), by_cell),
                pl.BlockSpec((per_step, slots, width, sw), lambda i, *_: (i, 0, 0, 0)),
            ],
            out_specs=[pl.BlockSpec((per_step, rows, width), by_cell)] + [summed] * 3
            + [pl.BlockSpec((n, rows, sw), whole, pipeline_mode=pl.Buffered(1)) for n in parts],
            scratch_shapes=[pltpu.VMEM((spans * blocks, rows, sw), F32)],
        ),
        compiler_params=pltpu.CompilerParams(vmem_limit_bytes=60 << 20),
        cost_estimate=pl.CostEstimate(flops=0, bytes_accessed=0, transcendentals=0),
        name="leaf",
    )(targets, right_side, leaf_inverse, leaf_couple)


def add_kernel(near_ref, *refs):
    *part_refs, out_ref = refs
    at = 0
    for ref in part_refs:
        count = ref.shape[0]
        mine = near_ref[pl.ds(at, count)].astype(F32)
        out_ref[pl.ds(at, count)] = (mine + ref[...].astype(F32)).astype(BF16)
        at += count


def add_parts(near, *parts):
    vmem = pl.BlockSpec(memory_space=pltpu.VMEM)
    return pl.pallas_call(
        add_kernel,
        out_shape=jax.ShapeDtypeStruct(near.shape, BF16),
        in_specs=[vmem] * (1 + len(parts)),
        out_specs=vmem,
        compiler_params=pltpu.CompilerParams(vmem_limit_bytes=16 << 20),
        cost_estimate=pl.CostEstimate(flops=0, bytes_accessed=0, transcendentals=0),
        name="add_parts",
    )(near, *parts)


def lift_kernel(base_ref, far_ref, near_ref, own_ref, prev_ref, next_ref, opp_lo_ref, opp_hi_ref, out_ref):
    blocks, rows, width = base_ref.shape
    sw = own_ref.shape[1]
    deep = opp_lo_ref.shape[0]
    depth = 2 * width
    column = lax.axis_index("rhs")
    total = jnp.zeros((rows, 4 * sw), F32)
    for b in range(0, blocks, 2):
        parts = [
            (base_ref[k] - far_ref[k].astype(F32) - near_ref[k].astype(F32)).astype(BF16) for k in (b, b + 1)
        ]
        row = b * width
        pieces = [ref[row : row + depth, :] for ref in (own_ref, prev_ref, next_ref)]
        opp_ref = (opp_lo_ref, opp_hi_ref)[row // deep]
        pieces.append(opp_ref[row % deep : row % deep + depth, :])
        total = total + dot32(jnp.concatenate(parts, axis=1), jnp.concatenate(pieces, axis=1))
    result = total.astype(BF16)
    for j, turn in enumerate((0, 3, 1, 2)):
        at = pl.multiple_of((column + turn) % 4 * sw, sw)
        out_ref[:, pl.ds(at, sw)] = result[:, j * sw : (j + 1) * sw]


def lift_phase(*operands):
    rows, cols = operands[0].shape[1], operands[3].shape[1]
    vmem = pl.BlockSpec(memory_space=pltpu.VMEM)
    return pl.pallas_call(
        lift_kernel,
        out_shape=jax.ShapeDtypeStruct((rows, 4 * cols), BF16),
        in_specs=[vmem] * len(operands),
        out_specs=vmem,
        compiler_params=pltpu.CompilerParams(vmem_limit_bytes=24 << 20),
        cost_estimate=pl.CostEstimate(flops=0, bytes_accessed=0, transcendentals=0),
        name="lift",
    )(*operands)


def assemble_kernel(with_product, own_ref, prev_ref, next_ref, opp_ref, ops_ref, *rest):
    sw = own_ref.shape[1]
    column = lax.axis_index("rhs")
    for turn, ref in ((0, own_ref), (3, prev_ref), (1, next_ref), (2, opp_ref)):
        ops_ref[:, pl.ds(pl.multiple_of((column + turn) % 4 * sw, sw), sw)] = ref[...]
    if with_product:
        (product_ref,) = rest
        width = ops_ref.shape[1]
        for r in range(0, 2 * width, width // 2):
            rows = pl.ds(r, width // 2)
            product_ref[rows, :] = (-dot32(ops_ref[rows, :], ops_ref[pl.ds(2 * width, width), :])).astype(BF16)


def assemble(pieces, with_product):
    depth, cols = pieces[0].shape
    outs = [jax.ShapeDtypeStruct((depth, 4 * cols), BF16)]
    if with_product:
        outs.append(jax.ShapeDtypeStruct((8 * cols, 4 * cols), BF16))
    vmem = pl.BlockSpec(memory_space=pltpu.VMEM)
    return pl.pallas_call(
        functools.partial(assemble_kernel, with_product),
        out_shape=tuple(outs),
        in_specs=[vmem] * 4,
        out_specs=tuple([vmem] * len(outs)),
        compiler_params=pltpu.CompilerParams(vmem_limit_bytes=16 << 20),
        cost_estimate=pl.CostEstimate(
            flops=0, bytes_accessed=0, transcendentals=0
        ),
        name="assemble_product" if with_product else "assemble",
    )(*pieces)


def top_kernel(first_ref, second_ref, ops_q_ref, ops_p_ref, sol_ref, skel_ref):
    width = first_ref.shape[1]

    def merge(first, second, ops_ref):
        sol = (dot32(first, ops_ref[pl.ds(0, width), :]) + dot32(second, ops_ref[pl.ds(width, width), :])).astype(BF16)
        skel = 0.5 * (first.astype(F32) + second.astype(F32)) - dot32(sol, ops_ref[pl.ds(2 * width, width), :])
        return sol, skel

    level_sol, level_skel = merge(first_ref[...], second_ref[...], ops_q_ref)
    sol, skel = merge(level_skel.astype(BF16), level_sol, ops_p_ref)
    sol_ref[...] = sol
    skel_ref[...] = skel


def top_phase(first, second, ops_q, ops_p):
    rows, width = first.shape
    vmem = pl.BlockSpec(memory_space=pltpu.VMEM)
    return pl.pallas_call(
        top_kernel,
        out_shape=(jax.ShapeDtypeStruct((rows, width), BF16), jax.ShapeDtypeStruct((rows, width), F32)),
        in_specs=[vmem] * 4,
        out_specs=(vmem, vmem),
        compiler_params=pltpu.CompilerParams(vmem_limit_bytes=16 << 20),
        cost_estimate=pl.CostEstimate(flops=400_000_000, bytes_accessed=4_000_000, transcendentals=0),
        name="top",
    )(first, second, ops_q, ops_p)


def on_device(
    right_side, leaf_inverse, leaf_couple, skel_target, skeleton_in, lift_ops, node_mix, node_couple
):
    count = lax.axis_size("cells")
    levels = count.bit_length() - 1
    rows, blocks, width = skeleton_in.shape

    lift = lift_ops[0]
    deep = lift.shape[0] // 2
    prev = shifted(lift, "rhs", 1)
    following = shifted(lift, "rhs", -1)

    solved, own, far, near, *parts = leaf_phase(skel_target, right_side, leaf_inverse, leaf_couple, blocks)

    half = range(count // 2)
    swap = [(2 * c, 2 * c + 1) for c in half] + [(2 * c + 1, 2 * c) for c in half]
    dest, red = parts[: len(DEST_PARTS)], parts[len(DEST_PARTS) :]
    red_in = [along_pairs(part, swap) for part in red]
    far_in = along_pairs(far, [(2 * c + 1, 2 * c + 3) for c in half] + [(2 * c, 2 * c - 2) for c in half])
    near = add_parts(near, *red_in)
    near_in = along_pairs(near, [(2 * c + 1, 2 * c + 2) for c in half] + [(2 * c, 2 * c - 1) for c in half])

    *dest, prev, following = lax.optimization_barrier((*dest, prev, following))
    opp_lo = shifted(prev[:deep], "rhs", 1)
    opp_hi = shifted(following[deep:], "rhs", -1)
    dest_in = jnp.concatenate([along_pairs(part, swap) for part in dest], axis=0)
    dest_in, far_in, near_in = lax.optimization_barrier((dest_in, far_in, near_in))
    base = lax.optimization_barrier(jnp.transpose(skeleton_in, (1, 0, 2)) - own - dest_in.astype(F32))
    current = lift_phase(base, far_in, near_in, lift, prev, following, opp_lo, opp_hi)
    base_after, far_after, near_after, _ = lax.optimization_barrier((base, far_in, near_in, current))
    skeleton_rhs = jnp.transpose(base_after - far_after.astype(F32) - near_after.astype(F32), (1, 0, 2))

    mix, couple, _ = lax.optimization_barrier((node_mix, node_couple, near))
    node_ops = jnp.concatenate([mix[0], couple[0]], axis=0)
    node_ops, _ = lax.optimization_barrier((node_ops, base))
    ops_prev = shifted(node_ops, "rhs", 1)
    ops_next = shifted(node_ops, "rhs", -1)
    node_ops, _, _ = lax.optimization_barrier((node_ops, opp_lo, opp_hi))
    across = shifted(node_ops, "cells", count // 2)
    ops_opp = shifted(node_ops, "rhs", 2)
    ops_p, product = assemble((node_ops, ops_prev, ops_next, ops_opp), True)

    mw = current.shape[1]
    for level in range(1, levels):
        distance = max(1, 2 ** (level - 2))
        first = shifted(current, "cells", distance)
        second = current if level == 1 else shifted(current, "cells", -distance)
        if level == 1:
            first, product, across = lax.optimization_barrier((first, product, across))
        if level == levels - 1:
            first, ops_q = lax.optimization_barrier((first, ops_q))
        skel = 0.5 * (first.astype(F32) + second.astype(F32)) + (
            dot32(first, product[:mw]) + dot32(second, product[mw:])
        )
        current = skel.astype(BF16)
        if level == 2:
            across, _ = lax.optimization_barrier((across, current))
            ops_q = assemble((across, *(shifted(across, "rhs", turn) for turn in (1, -1, 2))), False)[0]
    distance = 2 ** (levels - 2)
    second = shifted(current, "cells", distance)
    first = shifted(current, "cells", -distance)
    node_solution, node_skeleton = top_phase(first, second, ops_q, ops_p)
    return (solved, skeleton_rhs, node_solution[None], node_skeleton[None])


def solution(mesh):
    return jax.shard_map(
        on_device,
        mesh=mesh,
        in_specs=(
            P("cells", "rhs", None),
            P("cells", None, None),
            P("cells", None, None, None),
            P("cells", None),
            P("rhs", "cells", None),
            P("cells", None, "rhs"),
            P("cells", None, "rhs"),
            P("cells", None, "rhs"),
        ),
        out_specs=(
            P("cells", "rhs", None),
            P("rhs", "cells", None),
            P("cells", "rhs", None),
            P("cells", "rhs", None),
        ),
        check_vma=False,
    )
```

time: 162 us -> 128 us (0.79)
  the two profiles are of different devices: /device:TPU:1 before, /device:TPU:32 now
where the time goes in v2:
time: 128 us; the launch traced here: 127 us
  waiting for transfers between devices  57.8 us (45%)
  starting transfers between devices  46.4 us (36%)
  Pallas kernels  14.2 us (11%)
  local copies, waits for them, and re-layouts  3.86 us (3%)
  matrix products  2.33 us (2%)
  other arithmetic  1.99 us (2%)
    ppermute x22, waiting for transfers between devices, shifted(): lax.ppermute(value, axis, [(i, (i + by) % count) for i in range(count)])  48.3 us
    ppermute x22, starting transfers between devices, shifted(): lax.ppermute(value, axis, [(i, (i + by) % count) for i in range(count)])  39.4 us
    pallas_call x1, Pallas kernels, leaf_phase(): pl.pallas_call(functools.partial(leaf_kernel, per_step, slots, blocks), o...  10.2 us
    ppermute x6, waiting for transfers between devices, along_pairs(): lax.ppermute(value, 'cells', [(a, b) for a, b in pairs if 0 <= b < count])  9.56 us
    ppermute x6, starting transfers between devices, along_pairs(): lax.ppermute(value, 'cells', [(a, b) for a, b in pairs if 0 <= b < count])  6.97 us
    unnamed x17, local copies, waits for them, and re-layouts  3.79 us
  transfers between devices with their start and end apart: 28, of which 15 were waited for; matrix products, arithmetic and copies ran while one was open for 4% of the time, Pallas kernels for 10%

profile of v2, /device:TPU:32, one launch (start us, length us, event | category | flops | bytes accessed | tf_op | source)
XLA Modules:
  0.0 127.5 jit_solution(9677394133424674550)
XLA Ops:
  2.3 1.7 %collective-permute-start.1 = (bf16[4096,128]{1,0:T(8,128)(2,1)}, bf16[4096,128]{1,0:T(8,128)(2,1)S(1)}, u32[]{:S(2)}, u32[]{:S(2)}) collective-permute-start(bf16[4096,128]{1,0:T(8,128)(2,1)} %bitcast.22), channel_id=1, source_target_pairs={{0,3},{1,0},{2,1},{3,2},{4,7},{5,4},{6,5},{7,6},{8,11},{9,8},{10,9... | collective-permute-start | bytes 3145736 | tf_op jit(solution)/shard_map/ppermute | solution.py:23
  4.0 10.2 %leaf.1 = (bf16[8,128,384]{2,1,0:T(8,128)(2,1)}, f32[32,128,128]{2,1,0:T(8,128)}, bf16[32,128,128]{2,1,0:T(8,128)(2,1)}, bf16[32,128,128]{2,1,0:T(8,128)(2,1)}, ...) custom-call(s32[8,9]{1,0:T(8,128)} %target_ref.1, ...), custom_call_target="tpu_custom_call" | custom-call | tf_op jit(solution)/shard_map/leaf/pallas_call | solution.py:97
  14.6 3.7 %collective-permute-start.4 = (bf16[32,128,128]{2,1,0:T(8,128)(2,1)}, bf16[32,128,128]{2,1,0:T(8,128)(2,1)S(1)}, u32[]{:S(2)}, u32[]{:S(2)}) collective-permute-start(bf16[32,128,128]{2,1,0:T(8,128)(2,1)} %get-tuple-element.42), channel_id=1, source_target_pairs={{4,12},{12,20},{20,28},{28,36},{36,44},{44,52},{52,60},{60,68},{68... | collective-permute-start | bytes 3145736 | tf_op jit(solution)/shard_map/ppermute | solution.py:28
  19.9 2.2 %collective-permute-start.7 = (bf16[32,128,128]{2,1,0:T(8,128)(2,1)S(1)}, bf16[32,128,128]{2,1,0:T(8,128)(2,1)S(1)}, u32[]{:S(2)}, u32[]{:S(2)}) collective-permute-start(bf16[32,128,128]{2,1,0:T(8,128)(2,1)S(1)} %add_parts.1), channel_id=1, source_target_pairs={{4,8},{12,16},{20,24},{28,32},{36,40},{44,48},{52,56},{60,64},{68,... | collective-permute-start | bytes 3145736 | tf_op jit(solution)/shard_map/ppermute | solution.py:28
  22.1 5.0 %collective-permute-done.prev_ref = bf16[4096,128]{1,0:T(8,128)(2,1)S(1)} collective-permute-done((bf16[4096,128]{1,0:T(8,128)(2,1)}, bf16[4096,128]{1,0:T(8,128)(2,1)S(1)}, u32[]{:S(2)}, u32[]{:S(2)}) %collective-permute-start) | collective-permute-done | bytes 1048608 | tf_op jit(solution)/shard_map/ppermute | solution.py:23
  27.7 1.7 %collective-permute-start.8 = (bf16[2048,128]{1,0:T(8,128)(2,1)S(1)}, bf16[2048,128]{1,0:T(8,128)(2,1)S(1)}, u32[]{:S(2)}, u32[]{:S(2)}) collective-permute-start(bf16[2048,128]{1,0:T(8,128)(2,1)S(1)} %slice.8), channel_id=1, source_target_pairs={{0,1},{1,2},{2,3},{3,0},{4,5},{5,6},{6,7},{7,4},{8,9},{9,10},{10,1... | collective-permute-start | bytes 1572872 | tf_op jit(solution)/shard_map/ppermute | solution.py:23
  29.8 3.0 %collective-permute-start.9 = (bf16[2048,128]{1,0:T(8,128)(2,1)S(1)}, bf16[2048,128]{1,0:T(8,128)(2,1)S(1)}, u32[]{:S(2)}, u32[]{:S(2)}) collective-permute-start(bf16[2048,128]{1,0:T(8,128)(2,1)S(1)} %slice.9), channel_id=1, source_target_pairs={{0,3},{1,0},{2,1},{3,2},{4,7},{5,4},{6,5},{7,6},{8,11},{9,8},{10,9... | collective-permute-start | bytes 1572872 | tf_op jit(solution)/shard_map/ppermute | solution.py:23
  32.9 9.2 %collective-permute-done.7.near_ref = bf16[32,128,128]{2,1,0:T(8,128)(2,1)S(1)} collective-permute-done((bf16[32,128,128]{2,1,0:T(8,128)(2,1)S(1)}, bf16[32,128,128]{2,1,0:T(8,128)(2,1)S(1)}, u32[]{:S(2)}, u32[]{:S(2)}) %collective-permute-start.7) | collective-permute-done | bytes 1048608 | tf_op jit(solution)/shard_map/ppermute | solution.py:28
  43.7 3.1 %collective-permute-start.12 = (bf16[1536,128]{1,0:T(8,128)(2,1)S(1)}, bf16[1536,128]{1,0:T(8,128)(2,1)S(1)}, u32[]{:S(2)}, u32[]{:S(2)}) collective-permute-start(bf16[1536,128]{1,0:T(8,128)(2,1)S(1)} %pad_maximum_fusion.1.own_ref), channel_id=1, source_target_pairs={{0,3},{1,0},{2,1},{3,2},{4,7},{5,4},{6,5},{7,6},{8,11},{9,8},{10,9... | collective-permute-start | bytes 1179656 | tf_op jit(solution)/shard_map/ppermute | solution.py:23
  47.4 3.0 %collective-permute-start.14 = (bf16[1536,128]{1,0:T(8,128)(2,1)S(1)}, bf16[1536,128]{1,0:T(8,128)(2,1)S(1)}, u32[]{:S(2)}, u32[]{:S(2)}) collective-permute-start(bf16[1536,128]{1,0:T(8,128)(2,1)S(1)} %pad_maximum_fusion.1.own_ref), channel_id=1, source_target_pairs={{0,128},{4,132},{8,136},{12,140},{16,144},{20,148},{24,152},{28,15... | collective-permute-start | bytes 1179656 | tf_op jit(solution)/shard_map/ppermute | solution.py:23
  51.6 5.0 %collective-permute-done.11.prev_ref = bf16[1536,128]{1,0:T(8,128)(2,1)S(1)} collective-permute-done((bf16[1536,128]{1,0:T(8,128)(2,1)S(1)}, bf16[1536,128]{1,0:T(8,128)(2,1)S(1)}, u32[]{:S(2)}, u32[]{:S(2)}) %collective-permute-start.11) | collective-permute-done | bytes 393248 | tf_op jit(solution)/shard_map/ppermute | solution.py:23
  56.6 7.7 %collective-permute-done.12.next_ref = bf16[1536,128]{1,0:T(8,128)(2,1)S(1)} collective-permute-done((bf16[1536,128]{1,0:T(8,128)(2,1)S(1)}, bf16[1536,128]{1,0:T(8,128)(2,1)S(1)}, u32[]{:S(2)}, u32[]{:S(2)}) %collective-permute-start.12) | collective-permute-done | bytes 393248 | tf_op jit(solution)/shard_map/ppermute | solution.py:23
  67.2 2.0 %collective-permute-done.16 = bf16[128,512]{1,0:T(8,128)(2,1)S(1)} collective-permute-done((bf16[128,512]{1,0:T(8,128)(2,1)S(1)}, bf16[128,512]{1,0:T(8,128)(2,1)S(1)}, u32[]{:S(2)}, u32[]{:S(2)}) %collective-permute-start.16) | collective-permute-done | bytes 131104 | tf_op jit(solution)/shard_map/ppermute | solution.py:23
  69.4 1.7 %collective-permute-done.15 = bf16[128,512]{1,0:T(8,128)(2,1)S(1)} collective-permute-done((bf16[128,512]{1,0:T(8,128)(2,1)S(1)}, bf16[128,512]{1,0:T(8,128)(2,1)S(1)}, u32[]{:S(2)}, u32[]{:S(2)}) %collective-permute-start.15) | collective-permute-done | bytes 131104 | tf_op jit(solution)/shard_map/ppermute | solution.py:23
  71.4 4.2 %collective-permute-start.18 = (bf16[128,512]{1,0:T(8,128)(2,1)S(1)}, bf16[128,512]{1,0:T(8,128)(2,1)S(1)}, u32[]{:S(2)}, u32[]{:S(2)}) collective-permute-start(bf16[128,512]{1,0:T(8,128)(2,1)S(1)} %add_convert_fusion.3), channel_id=1, source_target_pairs={{0,248},{4,252},{8,0},{12,4},{16,8},{20,12},{24,16},{28,20},{32,24... | collective-permute-start | bytes 393224 | tf_op jit(solution)/shard_map/ppermute | solution.py:23
  75.6 2.5 %collective-permute-done.18 = bf16[128,512]{1,0:T(8,128)(2,1)S(1)} collective-permute-done((bf16[128,512]{1,0:T(8,128)(2,1)S(1)}, bf16[128,512]{1,0:T(8,128)(2,1)S(1)}, u32[]{:S(2)}, u32[]{:S(2)}) %collective-permute-start.18) | collective-permute-done | bytes 131104 | tf_op jit(solution)/shard_map/ppermute | solution.py:23
  78.4 4.9 %collective-permute-done.17 = bf16[128,512]{1,0:T(8,128)(2,1)S(1)} collective-permute-done((bf16[128,512]{1,0:T(8,128)(2,1)S(1)}, bf16[128,512]{1,0:T(8,128)(2,1)S(1)}, u32[]{:S(2)}, u32[]{:S(2)}) %collective-permute-start.17) | collective-permute-done | bytes 131104 | tf_op jit(solution)/shard_map/ppermute | solution.py:23
  83.5 5.1 %collective-permute-start.20 = (bf16[128,512]{1,0:T(8,128)(2,1)S(1)}, bf16[128,512]{1,0:T(8,128)(2,1)S(1)}, u32[]{:S(2)}, u32[]{:S(2)}) collective-permute-start(bf16[128,512]{1,0:T(8,128)(2,1)S(1)} %add_convert_fusion.2), channel_id=1, source_target_pairs={{0,240},{4,244},{8,248},{12,252},{16,0},{20,4},{24,8},{28,12},{32,... | collective-permute-start | bytes 393224 | tf_op jit(solution)/shard_map/ppermute | solution.py:23
  89.5 2.3 %collective-permute-start.23 = (bf16[1536,128]{1,0:T(8,128)(2,1)S(1)}, bf16[1536,128]{1,0:T(8,128)(2,1)S(1)}, u32[]{:S(2)}, u32[]{:S(2)}) collective-permute-start(bf16[1536,128]{1,0:T(8,128)(2,1)S(1)} %collective-permute-done.14.own_ref), channel_id=1, source_target_pairs={{0,3},{1,0},{2,1},{3,2},{4,7},{5,4},{6,5},{7,6},{8,11},{9,8},{10,9... | collective-permute-start | bytes 1179656 | tf_op jit(solution)/shard_map/ppermute | solution.py:23
  93.0 11.6 %collective-permute-done.19 = bf16[128,512]{1,0:T(8,128)(2,1)S(1)} collective-permute-done((bf16[128,512]{1,0:T(8,128)(2,1)S(1)}, bf16[128,512]{1,0:T(8,128)(2,1)S(1)}, u32[]{:S(2)}, u32[]{:S(2)}) %collective-permute-start.19) | collective-permute-done | bytes 131104 | tf_op jit(solution)/shard_map/ppermute | solution.py:23
  104.9 8.0 %collective-permute-start.25 = (bf16[128,512]{1,0:T(8,128)(2,1)S(1)}, bf16[128,512]{1,0:T(8,128)(2,1)S(1)}, u32[]{:S(2)}, u32[]{:S(2)}) collective-permute-start(bf16[128,512]{1,0:T(8,128)(2,1)S(1)} %add_convert_fusion.1), channel_id=1, source_target_pairs={{0,224},{4,228},{8,232},{12,236},{16,240},{20,244},{24,248},{28,25... | collective-permute-start | bytes 393224 | tf_op jit(solution)/shard_map/ppermute | solution.py:23
  113.3 3.3 %collective-permute-done.21 = bf16[128,512]{1,0:T(8,128)(2,1)S(1)} collective-permute-done((bf16[128,512]{1,0:T(8,128)(2,1)S(1)}, bf16[128,512]{1,0:T(8,128)(2,1)S(1)}, u32[]{:S(2)}, u32[]{:S(2)}) %collective-permute-start.21) | collective-permute-done | bytes 131104 | tf_op jit(solution)/shard_map/ppermute | solution.py:23
  121.2 2.5 %copy.13 = f32[128,32,128]{2,1,0:T(8,128)} copy(f32[128,32,128]{2,0,1:T(8,128)S(1)} %subtract_bitcast_fusion) | data formatting | bytes 4194304
  124.2 1.8 %collective-permute-done.27.second_ref = bf16[128,512]{1,0:T(8,128)(2,1)S(1)} collective-permute-done((bf16[128,512]{1,0:T(8,128)(2,1)S(1)}, bf16[128,512]{1,0:T(8,128)(2,1)S(1)}, u32[]{:S(2)}, u32[]{:S(2)}) %collective-permute-start.27) | collective-permute-done | bytes 131104 | tf_op jit(solution)/shard_map/ppermute | solution.py:23
  (71 shorter events, 21.1 us)
Async XLA Ops:
  0.6 26.5 %collective-permute-start = (bf16[4096,128]{1,0:T(8,128)(2,1)}, bf16[4096,128]{1,0:T(8,128)(2,1)S(1)}, u32[]{:S(2)}, u32[]{:S(2)}) collective-permute-start(bf16[4096,128]{1,0:T(8,128)(2,1)} %bitcast.21), channel_id=1, source_target_pairs={{0,1},{1,2},{2,3},{3,0},{4,5},{5,6},{6,7},{7,4},{8,9},{9,10},{10,1... | collective-permute-start | bytes 3145736 | tf_op jit(solution)/shard_map/ppermute | solution.py:23
  2.3 24.8 %collective-permute-start.1 = (bf16[4096,128]{1,0:T(8,128)(2,1)}, bf16[4096,128]{1,0:T(8,128)(2,1)S(1)}, u32[]{:S(2)}, u32[]{:S(2)}) collective-permute-start(bf16[4096,128]{1,0:T(8,128)(2,1)} %bitcast.22), channel_id=1, source_target_pairs={{0,3},{1,0},{2,1},{3,2},{4,7},{5,4},{6,5},{7,6},{8,11},{9,8},{10,9... | collective-permute-start | bytes 3145736 | tf_op jit(solution)/shard_map/ppermute | solution.py:23
  14.6 18.3 %collective-permute-start.4 = (bf16[32,128,128]{2,1,0:T(8,128)(2,1)}, bf16[32,128,128]{2,1,0:T(8,128)(2,1)S(1)}, u32[]{:S(2)}, u32[]{:S(2)}) collective-permute-start(bf16[32,128,128]{2,1,0:T(8,128)(2,1)} %get-tuple-element.42), channel_id=1, source_target_pairs={{4,12},{12,20},{20,28},{28,36},{36,44},{44,52},{52,60},{60,68},{68... | collective-permute-start | bytes 3145736 | tf_op jit(solution)/shard_map/ppermute | solution.py:28
  19.9 22.2 %collective-permute-start.7 = (bf16[32,128,128]{2,1,0:T(8,128)(2,1)S(1)}, bf16[32,128,128]{2,1,0:T(8,128)(2,1)S(1)}, u32[]{:S(2)}, u32[]{:S(2)}) collective-permute-start(bf16[32,128,128]{2,1,0:T(8,128)(2,1)S(1)} %add_parts.1), channel_id=1, source_target_pairs={{4,8},{12,16},{20,24},{28,32},{36,40},{44,48},{52,56},{60,64},{68,... | collective-permute-start | bytes 3145736 | tf_op jit(solution)/shard_map/ppermute | solution.py:28
  27.1 5.7 %collective-permute-start.2 = (bf16[24,128,128]{2,1,0:T(8,128)(2,1)S(1)}, bf16[24,128,128]{2,1,0:T(8,128)(2,1)S(1)}, u32[]{:S(2)}, u32[]{:S(2)}) collective-permute-start(bf16[24,128,128]{2,1,0:T(8,128)(2,1)S(1)} %copy-done.6), channel_id=1, source_target_pairs={{0,4},{8,12},{16,20},{24,28},{32,36},{40,44},{48,52},{56,60},{64,6... | collective-permute-start | bytes 2359304 | tf_op jit(solution)/shard_map/ppermute | solution.py:28
  27.7 19.1 %collective-permute-start.8 = (bf16[2048,128]{1,0:T(8,128)(2,1)S(1)}, bf16[2048,128]{1,0:T(8,128)(2,1)S(1)}, u32[]{:S(2)}, u32[]{:S(2)}) collective-permute-start(bf16[2048,128]{1,0:T(8,128)(2,1)S(1)} %slice.8), channel_id=1, source_target_pairs={{0,1},{1,2},{2,3},{3,0},{4,5},{5,6},{6,7},{7,4},{8,9},{9,10},{10,1... | collective-permute-start | bytes 1572872 | tf_op jit(solution)/shard_map/ppermute | solution.py:23
  29.8 17.1 %collective-permute-start.9 = (bf16[2048,128]{1,0:T(8,128)(2,1)S(1)}, bf16[2048,128]{1,0:T(8,128)(2,1)S(1)}, u32[]{:S(2)}, u32[]{:S(2)}) collective-permute-start(bf16[2048,128]{1,0:T(8,128)(2,1)S(1)} %slice.9), channel_id=1, source_target_pairs={{0,3},{1,0},{2,1},{3,2},{4,7},{5,4},{6,5},{7,6},{8,11},{9,8},{10,9... | collective-permute-start | bytes 1572872 | tf_op jit(solution)/shard_map/ppermute | solution.py:23
  43.5 13.1 %collective-permute-start.11 = (bf16[1536,128]{1,0:T(8,128)(2,1)S(1)}, bf16[1536,128]{1,0:T(8,128)(2,1)S(1)}, u32[]{:S(2)}, u32[]{:S(2)}) collective-permute-start(bf16[1536,128]{1,0:T(8,128)(2,1)S(1)} %pad_maximum_fusion.1.own_ref), channel_id=1, source_target_pairs={{0,1},{1,2},{2,3},{3,0},{4,5},{5,6},{6,7},{7,4},{8,9},{9,10},{10,1... | collective-permute-start | bytes 1179656 | tf_op jit(solution)/shard_map/ppermute | solution.py:23
  43.7 20.5 %collective-permute-start.12 = (bf16[1536,128]{1,0:T(8,128)(2,1)S(1)}, bf16[1536,128]{1,0:T(8,128)(2,1)S(1)}, u32[]{:S(2)}, u32[]{:S(2)}) collective-permute-start(bf16[1536,128]{1,0:T(8,128)(2,1)S(1)} %pad_maximum_fusion.1.own_ref), channel_id=1, source_target_pairs={{0,3},{1,0},{2,1},{3,2},{4,7},{5,4},{6,5},{7,6},{8,11},{9,8},{10,9... | collective-permute-start | bytes 1179656 | tf_op jit(solution)/shard_map/ppermute | solution.py:23
  46.8 18.2 %collective-permute-start.13 = (bf16[1536,128]{1,0:T(8,128)(2,1)S(1)}, bf16[1536,128]{1,0:T(8,128)(2,1)S(1)}, u32[]{:S(2)}, u32[]{:S(2)}) collective-permute-start(bf16[1536,128]{1,0:T(8,128)(2,1)S(1)} %pad_maximum_fusion.1.own_ref), channel_id=1, source_target_pairs={{0,2},{1,3},{2,0},{3,1},{4,6},{5,7},{6,4},{7,5},{8,10},{9,11},{10,... | collective-permute-start | bytes 1179656 | tf_op jit(solution)/shard_map/ppermute | solution.py:23
  47.4 18.7 %collective-permute-start.14 = (bf16[1536,128]{1,0:T(8,128)(2,1)S(1)}, bf16[1536,128]{1,0:T(8,128)(2,1)S(1)}, u32[]{:S(2)}, u32[]{:S(2)}) collective-permute-start(bf16[1536,128]{1,0:T(8,128)(2,1)S(1)} %pad_maximum_fusion.1.own_ref), channel_id=1, source_target_pairs={{0,128},{4,132},{8,136},{12,140},{16,144},{20,148},{24,152},{28,15... | collective-permute-start | bytes 1179656 | tf_op jit(solution)/shard_map/ppermute | solution.py:23
  51.3 14.8 %collective-permute-start.10 = (bf16[128,512]{1,0:T(8,128)(2,1)S(1)}, bf16[128,512]{1,0:T(8,128)(2,1)S(1)}, u32[]{:S(2)}, u32[]{:S(2)}) collective-permute-start(bf16[128,512]{1,0:T(8,128)(2,1)S(1)} %lift.1), channel_id=1, source_target_pairs={{0,4},{4,8},{8,12},{12,16},{16,20},{20,24},{24,28},{28,32},{32,36}... | collective-permute-start | bytes 393224 | tf_op jit(solution)/shard_map/ppermute | solution.py:23
  66.7 4.5 %collective-permute-start.15 = (bf16[128,512]{1,0:T(8,128)(2,1)S(1)}, bf16[128,512]{1,0:T(8,128)(2,1)S(1)}, u32[]{:S(2)}, u32[]{:S(2)}) collective-permute-start(bf16[128,512]{1,0:T(8,128)(2,1)S(1)} %add_convert_fusion.4), channel_id=1, source_target_pairs={{0,4},{4,8},{8,12},{12,16},{16,20},{20,24},{24,28},{28,32},{32,36}... | collective-permute-start | bytes 393224 | tf_op jit(solution)/shard_map/ppermute | solution.py:23
  71.4 6.7 %collective-permute-start.18 = (bf16[128,512]{1,0:T(8,128)(2,1)S(1)}, bf16[128,512]{1,0:T(8,128)(2,1)S(1)}, u32[]{:S(2)}, u32[]{:S(2)}) collective-permute-start(bf16[128,512]{1,0:T(8,128)(2,1)S(1)} %add_convert_fusion.3), channel_id=1, source_target_pairs={{0,248},{4,252},{8,0},{12,4},{16,8},{20,12},{24,16},{28,20},{32,24... | collective-permute-start | bytes 393224 | tf_op jit(solution)/shard_map/ppermute | solution.py:23
  75.6 7.6 %collective-permute-start.17 = (bf16[128,512]{1,0:T(8,128)(2,1)S(1)}, bf16[128,512]{1,0:T(8,128)(2,1)S(1)}, u32[]{:S(2)}, u32[]{:S(2)}) collective-permute-start(bf16[128,512]{1,0:T(8,128)(2,1)S(1)} %add_convert_fusion.3), channel_id=1, source_target_pairs={{0,8},{4,12},{8,16},{12,20},{16,24},{20,28},{24,32},{28,36},{32,40... | collective-permute-start | bytes 393224 | tf_op jit(solution)/shard_map/ppermute | solution.py:23
  83.5 9.3 %collective-permute-start.20 = (bf16[128,512]{1,0:T(8,128)(2,1)S(1)}, bf16[128,512]{1,0:T(8,128)(2,1)S(1)}, u32[]{:S(2)}, u32[]{:S(2)}) collective-permute-start(bf16[128,512]{1,0:T(8,128)(2,1)S(1)} %add_convert_fusion.2), channel_id=1, source_target_pairs={{0,240},{4,244},{8,248},{12,252},{16,0},{20,4},{24,8},{28,12},{32,... | collective-permute-start | bytes 393224 | tf_op jit(solution)/shard_map/ppermute | solution.py:23
  88.6 24.4 %collective-permute-start.22 = (bf16[1536,128]{1,0:T(8,128)(2,1)S(1)}, bf16[1536,128]{1,0:T(8,128)(2,1)S(1)}, u32[]{:S(2)}, u32[]{:S(2)}) collective-permute-start(bf16[1536,128]{1,0:T(8,128)(2,1)S(1)} %collective-permute-done.14.own_ref), channel_id=1, source_target_pairs={{0,1},{1,2},{2,3},{3,0},{4,5},{5,6},{6,7},{7,4},{8,9},{9,10},{10,1... | collective-permute-start | bytes 1179656 | tf_op jit(solution)/shard_map/ppermute | solution.py:23
  89.5 23.5 %collective-permute-start.23 = (bf16[1536,128]{1,0:T(8,128)(2,1)S(1)}, bf16[1536,128]{1,0:T(8,128)(2,1)S(1)}, u32[]{:S(2)}, u32[]{:S(2)}) collective-permute-start(bf16[1536,128]{1,0:T(8,128)(2,1)S(1)} %collective-permute-done.14.own_ref), channel_id=1, source_target_pairs={{0,3},{1,0},{2,1},{3,2},{4,7},{5,4},{6,5},{7,6},{8,11},{9,8},{10,9... | collective-permute-start | bytes 1179656 | tf_op jit(solution)/shard_map/ppermute | solution.py:23
  91.8 21.2 %collective-permute-start.24 = (bf16[1536,128]{1,0:T(8,128)(2,1)S(1)}, bf16[1536,128]{1,0:T(8,128)(2,1)S(1)}, u32[]{:S(2)}, u32[]{:S(2)}) collective-permute-start(bf16[1536,128]{1,0:T(8,128)(2,1)S(1)} %collective-permute-done.14.own_ref), channel_id=1, source_target_pairs={{0,2},{1,3},{2,0},{3,1},{4,6},{5,7},{6,4},{7,5},{8,10},{9,11},{10,... | collective-permute-start | bytes 1179656 | tf_op jit(solution)/shard_map/ppermute | solution.py:23
  92.8 11.8 %collective-permute-start.19 = (bf16[128,512]{1,0:T(8,128)(2,1)S(1)}, bf16[128,512]{1,0:T(8,128)(2,1)S(1)}, u32[]{:S(2)}, u32[]{:S(2)}) collective-permute-start(bf16[128,512]{1,0:T(8,128)(2,1)S(1)} %add_convert_fusion.2), channel_id=1, source_target_pairs={{0,16},{4,20},{8,24},{12,28},{16,32},{20,36},{24,40},{28,44},{32,4... | collective-permute-start | bytes 393224 | tf_op jit(solution)/shard_map/ppermute | solution.py:23
  104.8 11.7 %collective-permute-start.21 = (bf16[128,512]{1,0:T(8,128)(2,1)S(1)}, bf16[128,512]{1,0:T(8,128)(2,1)S(1)}, u32[]{:S(2)}, u32[]{:S(2)}) collective-permute-start(bf16[128,512]{1,0:T(8,128)(2,1)S(1)} %add_convert_fusion.1), channel_id=1, source_target_pairs={{0,32},{4,36},{8,40},{12,44},{16,48},{20,52},{24,56},{28,60},{32,6... | collective-permute-start | bytes 393224 | tf_op jit(solution)/shard_map/ppermute | solution.py:23
  104.9 13.2 %collective-permute-start.25 = (bf16[128,512]{1,0:T(8,128)(2,1)S(1)}, bf16[128,512]{1,0:T(8,128)(2,1)S(1)}, u32[]{:S(2)}, u32[]{:S(2)}) collective-permute-start(bf16[128,512]{1,0:T(8,128)(2,1)S(1)} %add_convert_fusion.1), channel_id=1, source_target_pairs={{0,224},{4,228},{8,232},{12,236},{16,240},{20,244},{24,248},{28,25... | collective-permute-start | bytes 393224 | tf_op jit(solution)/shard_map/ppermute | solution.py:23
  118.7 5.5 %collective-permute-start.26 = (bf16[128,512]{1,0:T(8,128)(2,1)S(1)}, bf16[128,512]{1,0:T(8,128)(2,1)S(1)}, u32[]{:S(2)}, u32[]{:S(2)}) collective-permute-start(bf16[128,512]{1,0:T(8,128)(2,1)S(1)} %add_convert_fusion), channel_id=1, source_target_pairs={{0,192},{4,196},{8,200},{12,204},{16,208},{20,212},{24,216},{28,22... | collective-permute-start | bytes 393224 | tf_op jit(solution)/shard_map/ppermute | solution.py:23
  119.3 6.6 %collective-permute-start.27 = (bf16[128,512]{1,0:T(8,128)(2,1)S(1)}, bf16[128,512]{1,0:T(8,128)(2,1)S(1)}, u32[]{:S(2)}, u32[]{:S(2)}) collective-permute-start(bf16[128,512]{1,0:T(8,128)(2,1)S(1)} %add_convert_fusion), channel_id=1, source_target_pairs={{0,64},{4,68},{8,72},{12,76},{16,80},{20,84},{24,88},{28,92},{32,9... | collective-permute-start | bytes 393224 | tf_op jit(solution)/shard_map/ppermute | solution.py:23
  (12 other events, 114.6 us)

commit v3 on v2

--- a/solution.py
+++ b/solution.py
@@ -276,8 +276,8 @@
     node_ops, _ = lax.optimization_barrier((node_ops, base))
     ops_prev = shifted(node_ops, "rhs", 1)
     ops_next = shifted(node_ops, "rhs", -1)
-    node_ops, _, _ = lax.optimization_barrier((node_ops, opp_lo, opp_hi))
-    across = shifted(node_ops, "cells", count // 2)
+    far_ops, _ = lax.optimization_barrier((node_ops, current))
+    across = shifted(far_ops, "cells", count // 2)
     ops_opp = shifted(node_ops, "rhs", 2)
     ops_p, product = assemble((node_ops, ops_prev, ops_next, ops_opp), True)
 

time: 128 us -> 128 us (level)
  no operation moved by 1% of the time
where the time goes in v3:
time: 128 us; the launch traced here: 127 us
  waiting for transfers between devices  56.9 us (44%)
  starting transfers between devices  47.2 us (37%)
  Pallas kernels  14.2 us (11%)
  local copies, waits for them, and re-layouts  3.86 us (3%)
  matrix products  2.32 us (2%)
  other arithmetic  1.99 us (2%)
    ppermute x22, waiting for transfers between devices, shifted(): lax.ppermute(value, axis, [(i, (i + by) % count) for i in range(count)])  47.3 us
    ppermute x22, starting transfers between devices, shifted(): lax.ppermute(value, axis, [(i, (i + by) % count) for i in range(count)])  40.3 us
    pallas_call x1, Pallas kernels, leaf_phase(): pl.pallas_call(functools.partial(leaf_kernel, per_step, slots, blocks), o...  10.2 us
    ppermute x6, waiting for transfers between devices, along_pairs(): lax.ppermute(value, 'cells', [(a, b) for a, b in pairs if 0 <= b < count])  9.56 us
    ppermute x6, starting transfers between devices, along_pairs(): lax.ppermute(value, 'cells', [(a, b) for a, b in pairs if 0 <= b < count])  6.97 us
    unnamed x17, local copies, waits for them, and re-layouts  3.79 us
  transfers between devices with their start and end apart: 28, of which 15 were waited for; matrix products, arithmetic and copies ran while one was open for 4% of the time, Pallas kernels for 10%

profile of v3, /device:TPU:32, one launch (start us, length us, event | category | flops | bytes accessed | tf_op | source)
XLA Modules:
  0.0 127.4 jit_solution(7242314505790120979)
XLA Ops:
  2.3 1.7 %collective-permute-start.1 = (bf16[4096,128]{1,0:T(8,128)(2,1)}, bf16[4096,128]{1,0:T(8,128)(2,1)S(1)}, u32[]{:S(2)}, u32[]{:S(2)}) collective-permute-start(bf16[4096,128]{1,0:T(8,128)(2,1)} %bitcast.22), channel_id=1, source_target_pairs={{0,3},{1,0},{2,1},{3,2},{4,7},{5,4},{6,5},{7,6},{8,11},{9,8},{10,9... | collective-permute-start | bytes 3145736 | tf_op jit(solution)/shard_map/ppermute | solution.py:23
  4.0 10.2 %leaf.1 = (bf16[8,128,384]{2,1,0:T(8,128)(2,1)}, f32[32,128,128]{2,1,0:T(8,128)}, bf16[32,128,128]{2,1,0:T(8,128)(2,1)}, bf16[32,128,128]{2,1,0:T(8,128)(2,1)}, ...) custom-call(s32[8,9]{1,0:T(8,128)} %target_ref.1, ...), custom_call_target="tpu_custom_call" | custom-call | tf_op jit(solution)/shard_map/leaf/pallas_call | solution.py:97
  14.6 3.7 %collective-permute-start.4 = (bf16[32,128,128]{2,1,0:T(8,128)(2,1)}, bf16[32,128,128]{2,1,0:T(8,128)(2,1)S(1)}, u32[]{:S(2)}, u32[]{:S(2)}) collective-permute-start(bf16[32,128,128]{2,1,0:T(8,128)(2,1)} %get-tuple-element.42), channel_id=1, source_target_pairs={{4,12},{12,20},{20,28},{28,36},{36,44},{44,52},{52,60},{60,68},{68... | collective-permute-start | bytes 3145736 | tf_op jit(solution)/shard_map/ppermute | solution.py:28
  19.9 2.2 %collective-permute-start.7 = (bf16[32,128,128]{2,1,0:T(8,128)(2,1)S(1)}, bf16[32,128,128]{2,1,0:T(8,128)(2,1)S(1)}, u32[]{:S(2)}, u32[]{:S(2)}) collective-permute-start(bf16[32,128,128]{2,1,0:T(8,128)(2,1)S(1)} %add_parts.1), channel_id=1, source_target_pairs={{4,8},{12,16},{20,24},{28,32},{36,40},{44,48},{52,56},{60,64},{68,... | collective-permute-start | bytes 3145736 | tf_op jit(solution)/shard_map/ppermute | solution.py:28
  22.1 5.0 %collective-permute-done.prev_ref = bf16[4096,128]{1,0:T(8,128)(2,1)S(1)} collective-permute-done((bf16[4096,128]{1,0:T(8,128)(2,1)}, bf16[4096,128]{1,0:T(8,128)(2,1)S(1)}, u32[]{:S(2)}, u32[]{:S(2)}) %collective-permute-start) | collective-permute-done | bytes 1048608 | tf_op jit(solution)/shard_map/ppermute | solution.py:23
  27.7 1.7 %collective-permute-start.8 = (bf16[2048,128]{1,0:T(8,128)(2,1)S(1)}, bf16[2048,128]{1,0:T(8,128)(2,1)S(1)}, u32[]{:S(2)}, u32[]{:S(2)}) collective-permute-start(bf16[2048,128]{1,0:T(8,128)(2,1)S(1)} %slice.8), channel_id=1, source_target_pairs={{0,1},{1,2},{2,3},{3,0},{4,5},{5,6},{6,7},{7,4},{8,9},{9,10},{10,1... | collective-permute-start | bytes 1572872 | tf_op jit(solution)/shard_map/ppermute | solution.py:23
  29.8 3.0 %collective-permute-start.9 = (bf16[2048,128]{1,0:T(8,128)(2,1)S(1)}, bf16[2048,128]{1,0:T(8,128)(2,1)S(1)}, u32[]{:S(2)}, u32[]{:S(2)}) collective-permute-start(bf16[2048,128]{1,0:T(8,128)(2,1)S(1)} %slice.9), channel_id=1, source_target_pairs={{0,3},{1,0},{2,1},{3,2},{4,7},{5,4},{6,5},{7,6},{8,11},{9,8},{10,9... | collective-permute-start | bytes 1572872 | tf_op jit(solution)/shard_map/ppermute | solution.py:23
  32.9 9.2 %collective-permute-done.7.near_ref = bf16[32,128,128]{2,1,0:T(8,128)(2,1)S(1)} collective-permute-done((bf16[32,128,128]{2,1,0:T(8,128)(2,1)S(1)}, bf16[32,128,128]{2,1,0:T(8,128)(2,1)S(1)}, u32[]{:S(2)}, u32[]{:S(2)}) %collective-permute-start.7) | collective-permute-done | bytes 1048608 | tf_op jit(solution)/shard_map/ppermute | solution.py:28
  43.7 3.1 %collective-permute-start.12 = (bf16[1536,128]{1,0:T(8,128)(2,1)S(1)}, bf16[1536,128]{1,0:T(8,128)(2,1)S(1)}, u32[]{:S(2)}, u32[]{:S(2)}) collective-permute-start(bf16[1536,128]{1,0:T(8,128)(2,1)S(1)} %pad_maximum_fusion.1.own_ref), channel_id=1, source_target_pairs={{0,3},{1,0},{2,1},{3,2},{4,7},{5,4},{6,5},{7,6},{8,11},{9,8},{10,9... | collective-permute-start | bytes 1179656 | tf_op jit(solution)/shard_map/ppermute | solution.py:23
  48.3 3.1 %collective-permute-start.14 = (bf16[1536,128]{1,0:T(8,128)(2,1)S(1)}, bf16[1536,128]{1,0:T(8,128)(2,1)S(1)}, u32[]{:S(2)}, u32[]{:S(2)}) collective-permute-start(bf16[1536,128]{1,0:T(8,128)(2,1)S(1)} %pad_maximum_fusion.1.own_ref), channel_id=1, source_target_pairs={{0,128},{4,132},{8,136},{12,140},{16,144},{20,148},{24,152},{28,15... | collective-permute-start | bytes 1179656 | tf_op jit(solution)/shard_map/ppermute | solution.py:23
  51.4 5.2 %collective-permute-done.11.prev_ref = bf16[1536,128]{1,0:T(8,128)(2,1)S(1)} collective-permute-done((bf16[1536,128]{1,0:T(8,128)(2,1)S(1)}, bf16[1536,128]{1,0:T(8,128)(2,1)S(1)}, u32[]{:S(2)}, u32[]{:S(2)}) %collective-permute-start.11) | collective-permute-done | bytes 393248 | tf_op jit(solution)/shard_map/ppermute | solution.py:23
  56.6 7.7 %collective-permute-done.12.next_ref = bf16[1536,128]{1,0:T(8,128)(2,1)S(1)} collective-permute-done((bf16[1536,128]{1,0:T(8,128)(2,1)S(1)}, bf16[1536,128]{1,0:T(8,128)(2,1)S(1)}, u32[]{:S(2)}, u32[]{:S(2)}) %collective-permute-start.12) | collective-permute-done | bytes 393248 | tf_op jit(solution)/shard_map/ppermute | solution.py:23
  67.2 2.0 %collective-permute-done.16 = bf16[128,512]{1,0:T(8,128)(2,1)S(1)} collective-permute-done((bf16[128,512]{1,0:T(8,128)(2,1)S(1)}, bf16[128,512]{1,0:T(8,128)(2,1)S(1)}, u32[]{:S(2)}, u32[]{:S(2)}) %collective-permute-start.16) | collective-permute-done | bytes 131104 | tf_op jit(solution)/shard_map/ppermute | solution.py:23
  69.4 1.7 %collective-permute-done.15 = bf16[128,512]{1,0:T(8,128)(2,1)S(1)} collective-permute-done((bf16[128,512]{1,0:T(8,128)(2,1)S(1)}, bf16[128,512]{1,0:T(8,128)(2,1)S(1)}, u32[]{:S(2)}, u32[]{:S(2)}) %collective-permute-start.15) | collective-permute-done | bytes 131104 | tf_op jit(solution)/shard_map/ppermute | solution.py:23
  71.4 5.2 %collective-permute-start.18 = (bf16[128,512]{1,0:T(8,128)(2,1)S(1)}, bf16[128,512]{1,0:T(8,128)(2,1)S(1)}, u32[]{:S(2)}, u32[]{:S(2)}) collective-permute-start(bf16[128,512]{1,0:T(8,128)(2,1)S(1)} %add_convert_fusion.3), channel_id=1, source_target_pairs={{0,248},{4,252},{8,0},{12,4},{16,8},{20,12},{24,16},{28,20},{32,24... | collective-permute-start | bytes 393224 | tf_op jit(solution)/shard_map/ppermute | solution.py:23
  76.7 2.5 %collective-permute-done.18 = bf16[128,512]{1,0:T(8,128)(2,1)S(1)} collective-permute-done((bf16[128,512]{1,0:T(8,128)(2,1)S(1)}, bf16[128,512]{1,0:T(8,128)(2,1)S(1)}, u32[]{:S(2)}, u32[]{:S(2)}) %collective-permute-start.18) | collective-permute-done | bytes 131104 | tf_op jit(solution)/shard_map/ppermute | solution.py:23
  79.4 3.8 %collective-permute-done.17 = bf16[128,512]{1,0:T(8,128)(2,1)S(1)} collective-permute-done((bf16[128,512]{1,0:T(8,128)(2,1)S(1)}, bf16[128,512]{1,0:T(8,128)(2,1)S(1)}, u32[]{:S(2)}, u32[]{:S(2)}) %collective-permute-start.17) | collective-permute-done | bytes 131104 | tf_op jit(solution)/shard_map/ppermute | solution.py:23
  83.5 5.1 %collective-permute-start.20 = (bf16[128,512]{1,0:T(8,128)(2,1)S(1)}, bf16[128,512]{1,0:T(8,128)(2,1)S(1)}, u32[]{:S(2)}, u32[]{:S(2)}) collective-permute-start(bf16[128,512]{1,0:T(8,128)(2,1)S(1)} %add_convert_fusion.2), channel_id=1, source_target_pairs={{0,240},{4,244},{8,248},{12,252},{16,0},{20,4},{24,8},{28,12},{32,... | collective-permute-start | bytes 393224 | tf_op jit(solution)/shard_map/ppermute | solution.py:23
  89.5 2.3 %collective-permute-start.23 = (bf16[1536,128]{1,0:T(8,128)(2,1)S(1)}, bf16[1536,128]{1,0:T(8,128)(2,1)S(1)}, u32[]{:S(2)}, u32[]{:S(2)}) collective-permute-start(bf16[1536,128]{1,0:T(8,128)(2,1)S(1)} %collective-permute-done.14.own_ref), channel_id=1, source_target_pairs={{0,3},{1,0},{2,1},{3,2},{4,7},{5,4},{6,5},{7,6},{8,11},{9,8},{10,9... | collective-permute-start | bytes 1179656 | tf_op jit(solution)/shard_map/ppermute | solution.py:23
  93.0 11.6 %collective-permute-done.19 = bf16[128,512]{1,0:T(8,128)(2,1)S(1)} collective-permute-done((bf16[128,512]{1,0:T(8,128)(2,1)S(1)}, bf16[128,512]{1,0:T(8,128)(2,1)S(1)}, u32[]{:S(2)}, u32[]{:S(2)}) %collective-permute-start.19) | collective-permute-done | bytes 131104 | tf_op jit(solution)/shard_map/ppermute | solution.py:23
  104.9 8.0 %collective-permute-start.25 = (bf16[128,512]{1,0:T(8,128)(2,1)S(1)}, bf16[128,512]{1,0:T(8,128)(2,1)S(1)}, u32[]{:S(2)}, u32[]{:S(2)}) collective-permute-start(bf16[128,512]{1,0:T(8,128)(2,1)S(1)} %add_convert_fusion.1), channel_id=1, source_target_pairs={{0,224},{4,228},{8,232},{12,236},{16,240},{20,244},{24,248},{28,25... | collective-permute-start | bytes 393224 | tf_op jit(solution)/shard_map/ppermute | solution.py:23
  113.3 3.3 %collective-permute-done.21 = bf16[128,512]{1,0:T(8,128)(2,1)S(1)} collective-permute-done((bf16[128,512]{1,0:T(8,128)(2,1)S(1)}, bf16[128,512]{1,0:T(8,128)(2,1)S(1)}, u32[]{:S(2)}, u32[]{:S(2)}) %collective-permute-start.21) | collective-permute-done | bytes 131104 | tf_op jit(solution)/shard_map/ppermute | solution.py:23
  121.2 2.5 %copy.13 = f32[128,32,128]{2,1,0:T(8,128)} copy(f32[128,32,128]{2,0,1:T(8,128)S(1)} %subtract_bitcast_fusion) | data formatting | bytes 4194304
  124.2 1.7 %collective-permute-done.27.second_ref = bf16[128,512]{1,0:T(8,128)(2,1)S(1)} collective-permute-done((bf16[128,512]{1,0:T(8,128)(2,1)S(1)}, bf16[128,512]{1,0:T(8,128)(2,1)S(1)}, u32[]{:S(2)}, u32[]{:S(2)}) %collective-permute-start.27) | collective-permute-done | bytes 131104 | tf_op jit(solution)/shard_map/ppermute | solution.py:23
  (71 shorter events, 20.9 us)
Async XLA Ops:
  0.6 26.5 %collective-permute-start = (bf16[4096,128]{1,0:T(8,128)(2,1)}, bf16[4096,128]{1,0:T(8,128)(2,1)S(1)}, u32[]{:S(2)}, u32[]{:S(2)}) collective-permute-start(bf16[4096,128]{1,0:T(8,128)(2,1)} %bitcast.21), channel_id=1, source_target_pairs={{0,1},{1,2},{2,3},{3,0},{4,5},{5,6},{6,7},{7,4},{8,9},{9,10},{10,1... | collective-permute-start | bytes 3145736 | tf_op jit(solution)/shard_map/ppermute | solution.py:23
  2.3 24.8 %collective-permute-start.1 = (bf16[4096,128]{1,0:T(8,128)(2,1)}, bf16[4096,128]{1,0:T(8,128)(2,1)S(1)}, u32[]{:S(2)}, u32[]{:S(2)}) collective-permute-start(bf16[4096,128]{1,0:T(8,128)(2,1)} %bitcast.22), channel_id=1, source_target_pairs={{0,3},{1,0},{2,1},{3,2},{4,7},{5,4},{6,5},{7,6},{8,11},{9,8},{10,9... | collective-permute-start | bytes 3145736 | tf_op jit(solution)/shard_map/ppermute | solution.py:23
  14.6 18.3 %collective-permute-start.4 = (bf16[32,128,128]{2,1,0:T(8,128)(2,1)}, bf16[32,128,128]{2,1,0:T(8,128)(2,1)S(1)}, u32[]{:S(2)}, u32[]{:S(2)}) collective-permute-start(bf16[32,128,128]{2,1,0:T(8,128)(2,1)} %get-tuple-element.42), channel_id=1, source_target_pairs={{4,12},{12,20},{20,28},{28,36},{36,44},{44,52},{52,60},{60,68},{68... | collective-permute-start | bytes 3145736 | tf_op jit(solution)/shard_map/ppermute | solution.py:28
  19.9 22.2 %collective-permute-start.7 = (bf16[32,128,128]{2,1,0:T(8,128)(2,1)S(1)}, bf16[32,128,128]{2,1,0:T(8,128)(2,1)S(1)}, u32[]{:S(2)}, u32[]{:S(2)}) collective-permute-start(bf16[32,128,128]{2,1,0:T(8,128)(2,1)S(1)} %add_parts.1), channel_id=1, source_target_pairs={{4,8},{12,16},{20,24},{28,32},{36,40},{44,48},{52,56},{60,64},{68,... | collective-permute-start | bytes 3145736 | tf_op jit(solution)/shard_map/ppermute | solution.py:28
  27.1 5.7 %collective-permute-start.2 = (bf16[24,128,128]{2,1,0:T(8,128)(2,1)S(1)}, bf16[24,128,128]{2,1,0:T(8,128)(2,1)S(1)}, u32[]{:S(2)}, u32[]{:S(2)}) collective-permute-start(bf16[24,128,128]{2,1,0:T(8,128)(2,1)S(1)} %copy-done.6), channel_id=1, source_target_pairs={{0,4},{8,12},{16,20},{24,28},{32,36},{40,44},{48,52},{56,60},{64,6... | collective-permute-start | bytes 2359304 | tf_op jit(solution)/shard_map/ppermute | solution.py:28
  27.7 19.6 %collective-permute-start.8 = (bf16[2048,128]{1,0:T(8,128)(2,1)S(1)}, bf16[2048,128]{1,0:T(8,128)(2,1)S(1)}, u32[]{:S(2)}, u32[]{:S(2)}) collective-permute-start(bf16[2048,128]{1,0:T(8,128)(2,1)S(1)} %slice.8), channel_id=1, source_target_pairs={{0,1},{1,2},{2,3},{3,0},{4,5},{5,6},{6,7},{7,4},{8,9},{9,10},{10,1... | collective-permute-start | bytes 1572872 | tf_op jit(solution)/shard_map/ppermute | solution.py:23
  29.8 17.6 %collective-permute-start.9 = (bf16[2048,128]{1,0:T(8,128)(2,1)S(1)}, bf16[2048,128]{1,0:T(8,128)(2,1)S(1)}, u32[]{:S(2)}, u32[]{:S(2)}) collective-permute-start(bf16[2048,128]{1,0:T(8,128)(2,1)S(1)} %slice.9), channel_id=1, source_target_pairs={{0,3},{1,0},{2,1},{3,2},{4,7},{5,4},{6,5},{7,6},{8,11},{9,8},{10,9... | collective-permute-start | bytes 1572872 | tf_op jit(solution)/shard_map/ppermute | solution.py:23
  43.5 13.1 %collective-permute-start.11 = (bf16[1536,128]{1,0:T(8,128)(2,1)S(1)}, bf16[1536,128]{1,0:T(8,128)(2,1)S(1)}, u32[]{:S(2)}, u32[]{:S(2)}) collective-permute-start(bf16[1536,128]{1,0:T(8,128)(2,1)S(1)} %pad_maximum_fusion.1.own_ref), channel_id=1, source_target_pairs={{0,1},{1,2},{2,3},{3,0},{4,5},{5,6},{6,7},{7,4},{8,9},{9,10},{10,1... | collective-permute-start | bytes 1179656 | tf_op jit(solution)/shard_map/ppermute | solution.py:23
  43.7 20.5 %collective-permute-start.12 = (bf16[1536,128]{1,0:T(8,128)(2,1)S(1)}, bf16[1536,128]{1,0:T(8,128)(2,1)S(1)}, u32[]{:S(2)}, u32[]{:S(2)}) collective-permute-start(bf16[1536,128]{1,0:T(8,128)(2,1)S(1)} %pad_maximum_fusion.1.own_ref), channel_id=1, source_target_pairs={{0,3},{1,0},{2,1},{3,2},{4,7},{5,4},{6,5},{7,6},{8,11},{9,8},{10,9... | collective-permute-start | bytes 1179656 | tf_op jit(solution)/shard_map/ppermute | solution.py:23
  46.8 18.2 %collective-permute-start.13 = (bf16[1536,128]{1,0:T(8,128)(2,1)S(1)}, bf16[1536,128]{1,0:T(8,128)(2,1)S(1)}, u32[]{:S(2)}, u32[]{:S(2)}) collective-permute-start(bf16[1536,128]{1,0:T(8,128)(2,1)S(1)} %pad_maximum_fusion.1.own_ref), channel_id=1, source_target_pairs={{0,2},{1,3},{2,0},{3,1},{4,6},{5,7},{6,4},{7,5},{8,10},{9,11},{10,... | collective-permute-start | bytes 1179656 | tf_op jit(solution)/shard_map/ppermute | solution.py:23
  48.3 17.8 %collective-permute-start.14 = (bf16[1536,128]{1,0:T(8,128)(2,1)S(1)}, bf16[1536,128]{1,0:T(8,128)(2,1)S(1)}, u32[]{:S(2)}, u32[]{:S(2)}) collective-permute-start(bf16[1536,128]{1,0:T(8,128)(2,1)S(1)} %pad_maximum_fusion.1.own_ref), channel_id=1, source_target_pairs={{0,128},{4,132},{8,136},{12,140},{16,144},{20,148},{24,152},{28,15... | collective-permute-start | bytes 1179656 | tf_op jit(solution)/shard_map/ppermute | solution.py:23
  51.4 14.7 %collective-permute-start.10 = (bf16[128,512]{1,0:T(8,128)(2,1)S(1)}, bf16[128,512]{1,0:T(8,128)(2,1)S(1)}, u32[]{:S(2)}, u32[]{:S(2)}) collective-permute-start(bf16[128,512]{1,0:T(8,128)(2,1)S(1)} %lift.1), channel_id=1, source_target_pairs={{0,4},{4,8},{8,12},{12,16},{16,20},{20,24},{24,28},{28,32},{32,36}... | collective-permute-start | bytes 393224 | tf_op jit(solution)/shard_map/ppermute | solution.py:23
  66.7 4.5 %collective-permute-start.15 = (bf16[128,512]{1,0:T(8,128)(2,1)S(1)}, bf16[128,512]{1,0:T(8,128)(2,1)S(1)}, u32[]{:S(2)}, u32[]{:S(2)}) collective-permute-start(bf16[128,512]{1,0:T(8,128)(2,1)S(1)} %add_convert_fusion.4), channel_id=1, source_target_pairs={{0,4},{4,8},{8,12},{12,16},{16,20},{20,24},{24,28},{28,32},{32,36}... | collective-permute-start | bytes 393224 | tf_op jit(solution)/shard_map/ppermute | solution.py:23
  71.4 7.8 %collective-permute-start.18 = (bf16[128,512]{1,0:T(8,128)(2,1)S(1)}, bf16[128,512]{1,0:T(8,128)(2,1)S(1)}, u32[]{:S(2)}, u32[]{:S(2)}) collective-permute-start(bf16[128,512]{1,0:T(8,128)(2,1)S(1)} %add_convert_fusion.3), channel_id=1, source_target_pairs={{0,248},{4,252},{8,0},{12,4},{16,8},{20,12},{24,16},{28,20},{32,24... | collective-permute-start | bytes 393224 | tf_op jit(solution)/shard_map/ppermute | solution.py:23
  76.7 6.6 %collective-permute-start.17 = (bf16[128,512]{1,0:T(8,128)(2,1)S(1)}, bf16[128,512]{1,0:T(8,128)(2,1)S(1)}, u32[]{:S(2)}, u32[]{:S(2)}) collective-permute-start(bf16[128,512]{1,0:T(8,128)(2,1)S(1)} %add_convert_fusion.3), channel_id=1, source_target_pairs={{0,8},{4,12},{8,16},{12,20},{16,24},{20,28},{24,32},{28,36},{32,40... | collective-permute-start | bytes 393224 | tf_op jit(solution)/shard_map/ppermute | solution.py:23
  83.5 9.3 %collective-permute-start.20 = (bf16[128,512]{1,0:T(8,128)(2,1)S(1)}, bf16[128,512]{1,0:T(8,128)(2,1)S(1)}, u32[]{:S(2)}, u32[]{:S(2)}) collective-permute-start(bf16[128,512]{1,0:T(8,128)(2,1)S(1)} %add_convert_fusion.2), channel_id=1, source_target_pairs={{0,240},{4,244},{8,248},{12,252},{16,0},{20,4},{24,8},{28,12},{32,... | collective-permute-start | bytes 393224 | tf_op jit(solution)/shard_map/ppermute | solution.py:23
  88.6 24.4 %collective-permute-start.22 = (bf16[1536,128]{1,0:T(8,128)(2,1)S(1)}, bf16[1536,128]{1,0:T(8,128)(2,1)S(1)}, u32[]{:S(2)}, u32[]{:S(2)}) collective-permute-start(bf16[1536,128]{1,0:T(8,128)(2,1)S(1)} %collective-permute-done.14.own_ref), channel_id=1, source_target_pairs={{0,1},{1,2},{2,3},{3,0},{4,5},{5,6},{6,7},{7,4},{8,9},{9,10},{10,1... | collective-permute-start | bytes 1179656 | tf_op jit(solution)/shard_map/ppermute | solution.py:23
  89.5 23.5 %collective-permute-start.23 = (bf16[1536,128]{1,0:T(8,128)(2,1)S(1)}, bf16[1536,128]{1,0:T(8,128)(2,1)S(1)}, u32[]{:S(2)}, u32[]{:S(2)}) collective-permute-start(bf16[1536,128]{1,0:T(8,128)(2,1)S(1)} %collective-permute-done.14.own_ref), channel_id=1, source_target_pairs={{0,3},{1,0},{2,1},{3,2},{4,7},{5,4},{6,5},{7,6},{8,11},{9,8},{10,9... | collective-permute-start | bytes 1179656 | tf_op jit(solution)/shard_map/ppermute | solution.py:23
  91.8 21.2 %collective-permute-start.24 = (bf16[1536,128]{1,0:T(8,128)(2,1)S(1)}, bf16[1536,128]{1,0:T(8,128)(2,1)S(1)}, u32[]{:S(2)}, u32[]{:S(2)}) collective-permute-start(bf16[1536,128]{1,0:T(8,128)(2,1)S(1)} %collective-permute-done.14.own_ref), channel_id=1, source_target_pairs={{0,2},{1,3},{2,0},{3,1},{4,6},{5,7},{6,4},{7,5},{8,10},{9,11},{10,... | collective-permute-start | bytes 1179656 | tf_op jit(solution)/shard_map/ppermute | solution.py:23
  92.8 11.8 %collective-permute-start.19 = (bf16[128,512]{1,0:T(8,128)(2,1)S(1)}, bf16[128,512]{1,0:T(8,128)(2,1)S(1)}, u32[]{:S(2)}, u32[]{:S(2)}) collective-permute-start(bf16[128,512]{1,0:T(8,128)(2,1)S(1)} %add_convert_fusion.2), channel_id=1, source_target_pairs={{0,16},{4,20},{8,24},{12,28},{16,32},{20,36},{24,40},{28,44},{32,4... | collective-permute-start | bytes 393224 | tf_op jit(solution)/shard_map/ppermute | solution.py:23
  104.8 11.7 %collective-permute-start.21 = (bf16[128,512]{1,0:T(8,128)(2,1)S(1)}, bf16[128,512]{1,0:T(8,128)(2,1)S(1)}, u32[]{:S(2)}, u32[]{:S(2)}) collective-permute-start(bf16[128,512]{1,0:T(8,128)(2,1)S(1)} %add_convert_fusion.1), channel_id=1, source_target_pairs={{0,32},{4,36},{8,40},{12,44},{16,48},{20,52},{24,56},{28,60},{32,6... | collective-permute-start | bytes 393224 | tf_op jit(solution)/shard_map/ppermute | solution.py:23
  104.9 13.2 %collective-permute-start.25 = (bf16[128,512]{1,0:T(8,128)(2,1)S(1)}, bf16[128,512]{1,0:T(8,128)(2,1)S(1)}, u32[]{:S(2)}, u32[]{:S(2)}) collective-permute-start(bf16[128,512]{1,0:T(8,128)(2,1)S(1)} %add_convert_fusion.1), channel_id=1, source_target_pairs={{0,224},{4,228},{8,232},{12,236},{16,240},{20,244},{24,248},{28,25... | collective-permute-start | bytes 393224 | tf_op jit(solution)/shard_map/ppermute | solution.py:23
  118.7 5.5 %collective-permute-start.26 = (bf16[128,512]{1,0:T(8,128)(2,1)S(1)}, bf16[128,512]{1,0:T(8,128)(2,1)S(1)}, u32[]{:S(2)}, u32[]{:S(2)}) collective-permute-start(bf16[128,512]{1,0:T(8,128)(2,1)S(1)} %add_convert_fusion), channel_id=1, source_target_pairs={{0,192},{4,196},{8,200},{12,204},{16,208},{20,212},{24,216},{28,22... | collective-permute-start | bytes 393224 | tf_op jit(solution)/shard_map/ppermute | solution.py:23
  119.2 6.6 %collective-permute-start.27 = (bf16[128,512]{1,0:T(8,128)(2,1)S(1)}, bf16[128,512]{1,0:T(8,128)(2,1)S(1)}, u32[]{:S(2)}, u32[]{:S(2)}) collective-permute-start(bf16[128,512]{1,0:T(8,128)(2,1)S(1)} %add_convert_fusion), channel_id=1, source_target_pairs={{0,64},{4,68},{8,72},{12,76},{16,80},{20,84},{24,88},{28,92},{32,9... | collective-permute-start | bytes 393224 | tf_op jit(solution)/shard_map/ppermute | solution.py:23
  (12 other events, 111.5 us)
